TPU v7x, 32 devices: a whole 2x2x4 slice. The times are simulated.
32 devices in a mesh: gx: 8 (over z, y), gy: 4 (over x, core).
Axes of the slice: x: 2, y: 2, z: 4, core: 2. Of those that a mesh axis runs over, the one named last changes fastest.
Arguments:
- charges: float32 [256, 128, 256], P('gx', 'gy'), may hold values from -6 to 6
- kernel_taps: float32 [3, 3, 21], replicated, may hold values from -1.08 to 1.08
Outputs:
- potential: float32 [256, 128, 256], P('gx', 'gy')
All inputs are finite; a program needn't handle non-finite values.
Results may differ from a plain program's by a relative error of at most 0.035.
Values sent between devices are 32-bit elements; how exact they have to be, the bound alone decides.
A program may use at most 128 MiB of HBM per device.

v0:
```python
import functools

import jax
import jax.numpy as jnp
import numpy as np
from jax import lax
from jax.experimental import pallas as pl
from jax.experimental.pallas import tpu as pltpu
from jax.sharding import PartitionSpec as P

SPLINE = (0.125, 0.5, 0.75, 0.5, 0.125)
F32, BF16 = jnp.float32, jnp.bfloat16
MESH = pl.DeviceIdType.MESH


def spline_at(offset):
    return SPLINE[offset + 2] if -2 <= offset <= 2 else 0.0


def fixed_table(rows, cols, width):
    table = np.zeros((width, len(cols)), np.float32)
    for a, fine in enumerate(rows):
        for b, other in enumerate(cols):
            if fine is not None and other is not None:
                table[a, b] = spline_at(other - 2 * fine)
    return table


def lifted_table(rows, cols, width):
    table = np.zeros((width, len(cols)), np.float32)
    for a, fine in enumerate(rows):
        for b, coarse in enumerate(cols):
            if coarse is not None:
                table[a, b] = spline_at(fine - 2 * coarse)
    return table


def twice(table):
    return jnp.asarray(np.concatenate([table, table], axis=1), BF16)


def halves(value):
    high = value.astype(BF16)
    return high, (value - high.astype(F32)).astype(BF16)


def dot(left, right):
    return jnp.dot(left, right, preferred_element_type=F32)


def stacked2(value):
    high, low = halves(value)
    return jnp.concatenate([high, low], axis=0)


def stacked3(value):
    high, low = halves(value)
    return jnp.concatenate([high, low, high], axis=0)


def repeat(count, step, body):
    def trip(i, carry):
        for k in range(step):
            body(i * step + k)
        return carry

    assert count % step == 0
    lax.fori_loop(0, count // step, trip, 0)


def kernel(nx, ny, radius, terms, taps, q, ry1, rz1, ry2, rz2, uy2, uz2, uy1, uz1, out,
           fine, mid, ext, got, left1, right1, low1, high1, l2w, cols2, seen2, strip2, far2, top,
           ty0, ty1, ty2, tz0, tz1, tz2, y0, s0, y1, s1, y2, s2, r1, l1w, l2y, tx, ty, md, my,
           send, recv):
    bx, by, bz = q.shape
    hx, hy, hz = bx // 2, by // 2, bz // 2
    ex, ey, ez = bx // 4, by // 4, bz // 4
    count = 2 * radius + 1
    margin = radius + 1
    me_x, me_y = lax.axis_index("gx"), lax.axis_index("gy")
    reach = 2
    wy = min(ny, 2 * reach + 1)
    low_y = -((wy - 1) // 2)

    def device(dx, dy):
        return {"gx": lax.rem(me_x + dx + nx, nx), "gy": lax.rem(me_y + dy + ny, ny)}

    peers = {}
    for dx, dy in [(-1, 0), (1, 0), (0, -1), (0, 1), (-2, 0), (2, 0)] + [
        (0, -(low_y + k)) for k in range(wy)
    ]:
        if dx % nx or dy % ny:
            peers[(dx % nx, dy % ny)] = (dx, dy)
    barrier = pltpu.get_barrier_semaphore()
    for dx, dy in peers.values():
        pl.semaphore_signal(barrier, inc=1, device_id=device(dx, dy), device_id_type=MESH)

    def tap(level, member, position):
        return taps[level, member, position]

    def band(level, member, rows, cols, first, cycle, places):
        column = lax.broadcasted_iota(jnp.int32, (rows, cols), 1)
        place = column
        for start, shift in places:
            place = jnp.where(column >= start, column + shift, place)
        offsets = place - lax.broadcasted_iota(jnp.int32, (rows, cols), 0) + first
        if cycle:
            offsets = jnp.where(offsets < 0, offsets + cycle, offsets)
            offsets = jnp.where(offsets >= cycle, offsets - cycle, offsets)
        table = jnp.zeros((rows, cols), F32)
        for position in range(count):
            table = jnp.where(offsets == position, tap(level, member, position), table)
        return table

    def y_table(ref, level, rows, cols, first, cycle, places):
        for member in range(terms):
            high, low = halves(band(level, member, rows, cols, first, cycle, places))
            at = slice(member * rows, (member + 1) * rows)
            ref[at, 0:cols] = high
            ref[at, cols : 2 * cols] = high
            ref[at, 2 * cols : 3 * cols] = low

    def z_table(ref, level, n):
        def rows_of(i):
            start = pl.multiple_of(i * 16, 16)
            offsets = (
                lax.broadcasted_iota(jnp.int32, (16, n), 0)
                + start
                - lax.broadcasted_iota(jnp.int32, (16, n), 1)
                + radius
            )
            offsets = jnp.where(offsets < 0, offsets + n, offsets)
            offsets = jnp.where(offsets >= n, offsets - n, offsets)
            for member in range(terms):
                table = jnp.zeros((16, n), F32)
                for position in range(count):
                    table = jnp.where(offsets == position, tap(level, member, position), table)
                high, low = halves(table)
                ref[0, pl.ds(pl.multiple_of(member * n + start, 16), 16), :] = high
                ref[1, pl.ds(pl.multiple_of(member * n + start, 16), 16), :] = low

        repeat(n // 16, 1, rows_of)

    sem = [0]

    def remote(source, target, dx, dy):
        index = sem[0]
        sem[0] += 1
        return pltpu.make_async_remote_copy(
            src_ref=source, dst_ref=target, send_sem=send.at[index], recv_sem=recv.at[index],
            device_id=device(dx, dy), device_id_type=MESH,
        )

    def both(copies):
        for copy in copies:
            copy.start()
        return copies

    def arrive(copies):
        for copy in copies:
            copy.wait_recv()

    x0, x1 = radius, radius + bx
    extra = radius - 8
    per = 8 // extra
    def weighted(source, i, low, high):
        total = None
        for k in range(-2, 3):
            if low <= 2 * i + k < high:
                piece = source(2 * i + k) * SPLINE[k + 2]
                total = piece if total is None else total + piece
        return total

    rows1, rows2 = hx + 2, ex + 3
    wide1, wide2 = ry1.shape[0], ry2.shape[0]
    for i in range(rows1):
        r1[i] = dot(ry1[...], stacked2(weighted(lambda f: q[f], i - 1, 0, bx)))
    high, low = halves(r1[...].reshape(rows1 * wide1, bz))
    l1w[...] = (dot(high, rz1[...]) + dot(low, rz1[...])).reshape(rows1, wide1, hz)
    for i in range(rows2):
        l2y[i] = dot(ry2[...], stacked2(weighted(lambda f: l1w[f + 1], i - 1, -1, hx + 1)))
    high, low = halves(l2y[...].reshape(rows2 * wide2, hz))
    l2w[...] = (dot(high, rz2[...]) + dot(low, rz2[...])).reshape(rows2, wide2, ez)
    pl.semaphore_wait(barrier, len(peers))
    spot = -low_y
    fan = both([
        remote(l2w, cols2.at[k], 0, -(low_y + k)) for k in range(wy) if low_y + k
    ])
    rim = both([
        remote(l1w.at[rows1 - margin - 1 : rows1], low1, 1, 0),
        remote(l1w.at[0 : margin + 1], high1, -1, 0),
    ])
    g1 = bx // per
    side = both([
        remote(q.at[:, by - 8 : by], fine.at[x0:x1, by : by + 8], 0, 1),
        remote(q.at[:, 0:8], fine.at[x0:x1, by + 8 : by + 16], 0, -1),
    ])
    for i in range(bx):
        g, r = i // per, extra * (i % per)
        ext[0, g, r : r + extra] = q[i, by - radius : by - 8]
        ext[1, g, r : r + extra] = q[i, 8:radius]

    side += both([
        remote(ext.at[0, 0:g1], got.at[0, 0:g1], 0, 1),
        remote(ext.at[1, 0:g1], got.at[1, 0:g1], 0, -1),
    ])
    y_table(ty2, 2, wide2, wy * ey, low_y * ey + 1 + radius, wy * ey if ny <= 2 * reach + 1 else 0, [])
    z_table(tz2, 2, ez)

    cols2[spot] = l2w[...]
    arrive(fan)
    for k in range(wy):
        strip2[:, k * ey : (k + 1) * ey, :] = cols2[k, :, 0:ey, :]
    for k in range(wy):
        for at, place in ((ey, (k + 1) * ey), (ey + 1, (k + 1) * ey + 1), (ey + 2, k * ey - 1)):
            if ny <= 2 * reach + 1:
                place %= wy * ey
            if 0 <= place < wy * ey:
                strip2[:, place : place + 1, :] += cols2[k, :, at : at + 1, :]
    tail = margin - ex + 2
    lines = both([
        remote(strip2, seen2.at[0], 1, 0),
        remote(strip2, seen2.at[1], -1, 0),
        remote(strip2.at[rows2 - tail : rows2], far2.at[0], 2, 0),
        remote(strip2.at[0:tail], far2.at[1], -2, 0),
    ])
    far = both([
        remote(q.at[bx - radius : bx], fine.at[0:x0, 0:by], 1, 0),
        remote(q.at[0:radius], fine.at[x1 : x1 + radius, 0:by], -1, 0),
    ])
    fine[x0:x1, 0:by, :] = q[...]
    y_table(ty0, 0, by, by + 24, radius, 0, [(by, -by - 8), (by + 8, -8), (by + 16, -by - 16 - radius), (by + 16 + extra, -8 - extra), (by + 16 + 2 * extra, 1000)])
    y_table(ty1, 1, wide1, wide1 + 2 * hy, radius + 1, 0, [(hy + 1, -hy - 2), (hy + 2, 1000), (wide1, -wide1 - hy + 1), (wide1 + hy, -wide1 - 1)])
    z_table(tz0, 0, bz)
    spare = jnp.zeros((8 - 2 * extra, bz), F32)

    def unpack(rows, first):
        for n, i in enumerate(rows):
            g, r = first + n // per, extra * (n % per)
            fine[i, by + 16 : by + 16 + extra] = got[0, g, r : r + extra]
            fine[i, by + 16 + extra : by + 16 + 2 * extra] = got[1, g, r : r + extra]
            fine[i, by + 16 + 2 * extra : by + 24] = spare

    z_table(tz1, 1, hz)

    arrive(rim)
    mid[0 : margin + 1, 0:wide1] = low1[...]
    mid[margin + 1 : margin + hx - 1, 0:wide1] = l1w[2:hx]
    mid[margin + hx - 1 : margin + hx + margin, 0:wide1] = high1[...]
    for i, j in ((margin - 1, 0), (margin, 1), (margin + hx - 1, hx), (margin + hx, hx + 1)):
        mid[i, 0:wide1] += l1w[j]
    left1[...] = mid[:, 1 : hy + 1, :]
    right1[:, 0:1, :] = mid[:, hy + 1 : hy + 2, :]
    right1[:, 1:hy, :] = mid[:, 0 : hy - 1, :]
    rim2 = both([
        remote(left1, mid.at[:, wide1 : wide1 + hy], 0, 1),
        remote(right1, mid.at[:, wide1 + hy : wide1 + 2 * hy], 0, -1),
    ])
    outer = list(range(x0)) + list(range(x1, x1 + radius))
    def correlate_y(ref, source, table, rows, step, first=0):
        width = table.shape[0] // terms

        def one(i):
            i = i + first
            value = dot(table[...], stacked3(source[i]))
            for member in range(terms):
                ref[member, i] = value[member * width : (member + 1) * width]

        repeat(rows, step, one)

    def correlate_x(ref, source, level, rows, first, step, start=0):
        def one(i):
            i = i + start
            for member in range(terms):
                total = None
                for position in range(count):
                    piece = source[member, i + first + position] * tap(level, member, position)
                    total = piece if total is None else total + piece
                high, low = halves(total)
                at = slice(member * total.shape[1], (member + 1) * total.shape[1])
                ref[0, i, :, at] = high
                ref[1, i, :, at] = low

        repeat(rows, step, one)

    def correlate_z(ref, table, a, b):
        size = (b - a) * ref.shape[2]
        high = ref[0, a:b].reshape(size, ref.shape[3])
        low = ref[1, a:b].reshape(size, ref.shape[3])
        return dot(high, table[0]) + dot(low, table[0]) + dot(high, table[1])

    def prolong_x(source, j, first):
        at = j - 2 * first
        if j % 2 == 0:
            c = (j // 2) - first
            return source[c - 1] * 0.125 + source[c] * 0.75 + source[c + 1] * 0.125
        c = (j - 1) // 2 - first
        return source[c] * 0.5 + source[c + 1] * 0.5

    arrive(side)
    unpack(range(x0, x1), 0)
    correlate_y(y0, fine, ty0, bx, 4, x0)

    arrive(lines)
    top[...] = jnp.zeros(top.shape, F32)
    home = radius
    for first, source in ((home, strip2), (home - ex, seen2.at[0]), (home + ex, seen2.at[1])):
        top[first : first + rows2] += source[...]
    top[0:tail] += far2[0]
    top[home + 2 * ex : home + 2 * ex + tail] += far2[1]
    correlate_y(y2, top, ty2, top.shape[0], top.shape[0])
    correlate_x(s2, y2, 2, rows2, 0, 1)
    tx[...] = correlate_z(s2, tz2, 0, rows2).reshape(tx.shape)
    for j in range(hx + 2):
        ty[j] = dot(uy2[...], stacked2(prolong_x(tx, j - 1, -1)))
    high, low = halves(ty[...].reshape((hx + 2) * ty.shape[1], ez))
    lifted = dot(high, uz2[...]) + dot(low, uz2[...])

    md[...] = lifted.reshape(md.shape)
    arrive(rim2)
    correlate_y(y1, mid, ty1, hx + 2 * margin, 2)
    correlate_x(s1, y1, 1, hx + 2, 0, 1)
    md[...] += correlate_z(s1, tz1, 0, hx + 2).reshape(md.shape)
    for j in range(bx):
        high, low = halves(dot(uy1[...], stacked2(prolong_x(md, j, -1))))
        my[0, j] = high
        my[1, j] = low

    def finish(a, b):
        high = my[0, a:b].reshape((b - a) * by, hz)
        low = my[1, a:b].reshape((b - a) * by, hz)
        total = correlate_z(s0, tz0, a, b) + dot(high, uz1[...]) + dot(low, uz1[...])
        out[a:b] = total.reshape(b - a, by, bz)

    correlate_x(s0, y0, 0, bx - 2 * radius, 0, 1, radius)
    finish(radius, bx - radius)
    arrive(far)
    for n, i in enumerate(outer):
        g, r = g1 + n // per, extra * (n % per)
        ext[0, g, r : r + extra] = fine[i, by - radius : by - 8, :]
        ext[1, g, r : r + extra] = fine[i, 8:radius, :]
    g2 = ext.shape[1]
    corner = both(
        [remote(fine.at[a:b, by - 8 : by], fine.at[a:b, by : by + 8], 0, 1) for a, b in ((0, x0), (x1, x1 + radius))]
        + [remote(fine.at[a:b, 0:8], fine.at[a:b, by + 8 : by + 16], 0, -1) for a, b in ((0, x0), (x1, x1 + radius))]
        + [remote(ext.at[0, g1:g2], got.at[0, g1:g2], 0, 1), remote(ext.at[1, g1:g2], got.at[1, g1:g2], 0, -1)]
    )

    arrive(corner)
    unpack(outer, g1)
    correlate_y(y0, fine, ty0, x0, 5)
    correlate_y(y0, fine, ty0, radius, 5, x1)
    correlate_x(s0, y0, 0, radius, 0, 1)
    correlate_x(s0, y0, 0, radius, 0, 1, bx - radius)
    finish(0, radius)
    finish(bx - radius, bx)
    for copy in fan + rim + side + lines + far + rim2 + corner:
        copy.wait_send()


def cyclic_restrict(n):
    rows = np.arange(n)[:, None]
    cols = np.arange(n // 2)[None, :]
    table = np.zeros((n, n // 2), np.float32)
    for k in range(-2, 3):
        table += SPLINE[k + 2] * ((2 * cols + k) % n == rows)
    return table


def body(charges, kernel_taps):
    nx, ny = lax.axis_size("gx"), lax.axis_size("gy")
    levels, terms, count = kernel_taps.shape
    radius = count // 2
    margin = radius + 1
    bx, by, bz = charges.shape
    hx, hy, hz = bx // 2, by // 2, bz // 2
    ex, ey, ez = bx // 4, by // 4, bz // 4
    pad = 16
    wy = min(ny, 5)
    order1 = list(range(hy)) + [hy, -1] + [None] * 6
    ry1 = fixed_table(order1, list(range(by)), len(order1))
    order2 = list(range(ey)) + [ey, ey + 1, -1] + [None] * 5
    ry2 = fixed_table(order2, order1, len(order2))
    rz1, rz2 = cyclic_restrict(bz), cyclic_restrict(hz)
    wide1 = hy + 8
    wide2 = ey + 8
    uy2 = lifted_table(list(range(-1, hy + 1)), list(range(-1, ey + 2)) + [None] * (wide2 - ey - 3), wide1)
    uy1 = lifted_table(list(range(by)), list(range(-1, hy + 1)) + [None] * (wide1 - hy - 2), by)
    fixed = [twice(ry1), jnp.asarray(rz1, BF16), twice(ry2), jnp.asarray(rz2, BF16), twice(uy2),
             jnp.asarray(rz2.T, BF16), twice(uy1), jnp.asarray(rz1.T, BF16)]
    rows1, rows2 = hx + 2, ex + 3
    extra = radius - 8
    packed = -(-(bx + 2 * radius) * extra // 8)
    scratch = [
        pltpu.VMEM(shape, dtype)
        for shape, dtype in (
            ((bx + 2 * radius, by + 24, bz), F32),
            ((hx + 2 * margin, wide1 + 2 * hy, hz), F32),
            ((2, packed, 8, bz), F32),
            ((2, packed, 8, bz), F32),
            ((hx + 2 * margin, hy, hz), F32),
            ((hx + 2 * margin, hy, hz), F32),
            ((margin + 1, wide1, hz), F32),
            ((margin + 1, wide1, hz), F32),
            ((rows2, wide2, ez), F32),
            ((wy, rows2, wide2, ez), F32),
            ((2, rows2, wy * ey, ez), F32),
            ((rows2, wy * ey, ez), F32),
            ((2, margin - ex + 2, wy * ey, ez), F32),
            ((rows2 + 2 * radius, wy * ey, ez), F32),
            ((terms * by, 3 * (by + 24)), BF16),
            ((terms * wide1, 3 * (wide1 + 2 * hy)), BF16),
            ((terms * wide2, 3 * wy * ey), BF16),
            ((2, terms * bz, bz), BF16),
            ((2, terms * hz, hz), BF16),
            ((2, terms * ez, ez), BF16),
            ((terms, bx + 2 * radius, by, bz), F32),
            ((2, bx, by, terms * bz), BF16),
            ((terms, hx + 2 * margin, wide1, hz), F32),
            ((2, hx + 2, wide1, terms * hz), BF16),
            ((terms, rows2 + 2 * radius, wide2, ez), F32),
            ((2, rows2, wide2, terms * ez), BF16),
            ((rows1, wide1, bz), F32),
            ((rows1, wide1, hz), F32),
            ((rows2, wide2, hz), F32),
            ((rows2, wide2, ez), F32),
            ((hx + 2, wide1, ez), F32),
            ((hx + 2, wide1, hz), F32),
            ((2, bx, by, hz), BF16),
        )
    ] + [
        pltpu.SemaphoreType.DMA((48,)),
        pltpu.SemaphoreType.DMA((48,)),
    ]
    return pl.pallas_call(
        functools.partial(kernel, nx, ny, radius, terms),
        out_shape=jax.ShapeDtypeStruct(charges.shape, F32),
        in_specs=[pl.BlockSpec(memory_space=pltpu.SMEM)] + [pl.BlockSpec(memory_space=pltpu.VMEM)] * 9,
        out_specs=pl.BlockSpec(memory_space=pltpu.VMEM),
        scratch_shapes=scratch,
        compiler_params=pltpu.CompilerParams(
            collective_id=0, has_side_effects=True, vmem_limit_bytes=60 * 2**20
        ),
    )(kernel_taps, charges, *fixed)


def solution(mesh):
    return jax.shard_map(
        body,
        mesh=mesh,
        in_specs=(P("gx", "gy", None), P()),
        out_specs=P("gx", "gy", None),
        check_vma=False,
    )
```

profile of v0, /device:TPU:1, one launch (start us, length us, event | category | flops | bytes accessed | tf_op | source)
XLA Modules:
  0.0 55.0 jit_solution(12701041701118754324)
XLA Ops:
  0.0 52.7 %shard_map.100 = f32[32,32,256]{2,1,0:T(8,128)} custom-call(f32[3,3,21]{2,1,0:T(4,128)} %taps.1, f32[32,32,256]{2,1,0:T(8,128)} %q.1, bf16[24,64]{1,0:T(8,128)(2,1)} %constant.16.clone.ry1, bf16[256,128]{1,0:T(8,128)(2,1)} %constant.17.clone.rz1, bf16[16,48]{1,0:T(8,128)(2,1)} %constant.18.clone.ry2, bf16[128,64]{1,0:T(8,128)(2,1)} %constant.19.clone.rz2, ...), custom_call_target="tpu_custom_call" | custom-call | tf_op jit(solution)/shard_map/pallas_call | solution.py:435
  52.7 2.3 %copy.12 = f32[32,32,256]{2,1,0:T(8,128)} copy(f32[32,32,256]{2,1,0:T(8,128)} %shard_map.100) | data formatting | bytes 2097152
where the time goes:
time: 55.2 us; the launch traced here: 55 us
  Pallas kernels  52.7 us (95%)
  local copies, waits for them, and re-layouts  2.31 us (4%)
    pallas_call x1, Pallas kernels, body(): pl.pallas_call(functools.partial(kernel, nx, ny, radius, terms), out_shap...  52.7 us
    unnamed x1, local copies, waits for them, and re-layouts  2.31 us

commit v1 on v0

--- a/solution.py
+++ b/solution.py
@@ -69,7 +69,7 @@
 
 
 def kernel(nx, ny, radius, terms, taps, q, ry1, rz1, ry2, rz2, uy2, uz2, uy1, uz1, out,
-           fine, mid, ext, got, left1, right1, low1, high1, l2w, cols2, seen2, strip2, far2, top,
+           fine, mid, ext, got, left1, right1, low1, high1, l2p, cols2, seen2, top,
            ty0, ty1, ty2, tz0, tz1, tz2, y0, s0, y1, s1, y2, s2, r1, l1w, l2y, tx, ty, md, my,
            send, recv):
     bx, by, bz = q.shape
@@ -79,6 +79,8 @@
     margin = radius + 1
     me_x, me_y = lax.axis_index("gx"), lax.axis_index("gy")
     reach = 2
+    odd = lax.rem(me_x, 2) if nx % 2 == 0 else 0
+    even = 1 - odd
     wy = min(ny, 2 * reach + 1)
     low_y = -((wy - 1) // 2)
 
@@ -172,6 +174,7 @@
         return total
 
     rows1, rows2 = hx + 2, ex + 3
+    half2 = l2p.shape[0]
     wide1, wide2 = ry1.shape[0], ry2.shape[0]
     for i in range(rows1):
         r1[i] = dot(ry1[...], stacked2(weighted(lambda f: q[f], i - 1, 0, bx)))
@@ -179,18 +182,24 @@
     l1w[...] = (dot(high, rz1[...]) + dot(low, rz1[...])).reshape(rows1, wide1, hz)
     for i in range(rows2):
         l2y[i] = dot(ry2[...], stacked2(weighted(lambda f: l1w[f + 1], i - 1, -1, hx + 1)))
-    high, low = halves(l2y[...].reshape(rows2 * wide2, hz))
-    l2w[...] = (dot(high, rz2[...]) + dot(low, rz2[...])).reshape(rows2, wide2, ez)
+    for i in range(rows2, 2 * half2):
+        l2y[i] = jnp.zeros((wide2, hz), F32)
+    high, low = halves(jnp.concatenate([l2y[0:half2], l2y[half2 : 2 * half2]], axis=2).reshape(half2 * wide2, 2 * hz))
+    l2p[...] = (dot(high, rz2[...]) + dot(low, rz2[...])).reshape(l2p.shape)
     pl.semaphore_wait(barrier, len(peers))
     spot = -low_y
-    fan = both([
-        remote(l2w, cols2.at[k], 0, -(low_y + k)) for k in range(wy) if low_y + k
+    lines = both([
+        remote(l2p, seen2.at[0], 1, 0),
+        remote(l2p, seen2.at[1], -1, 0),
+        remote(l2p, seen2.at[2], 2, 0),
+        remote(l2p, seen2.at[3], -2, 0),
     ])
     rim = both([
         remote(l1w.at[rows1 - margin - 1 : rows1], low1, 1, 0),
         remote(l1w.at[0 : margin + 1], high1, -1, 0),
     ])
     g1 = bx // per
+    steps = near_steps(radius)
     side = both([
         remote(q.at[:, by - 8 : by], fine.at[x0:x1, by : by + 8], 0, 1),
         remote(q.at[:, 0:8], fine.at[x0:x1, by + 8 : by + 16], 0, -1),
@@ -204,30 +213,22 @@
         remote(ext.at[0, 0:g1], got.at[0, 0:g1], 0, 1),
         remote(ext.at[1, 0:g1], got.at[1, 0:g1], 0, -1),
     ])
-    y_table(ty2, 2, wide2, wy * ey, low_y * ey + 1 + radius, wy * ey if ny <= 2 * reach + 1 else 0, [])
+    def pick(first, second):
+        return even * first + odd * second
+
+    def span(start, size):
+        return pl.ds(start, size)
+
+    near = [
+        both([remote(q.at[span(pick(bx - b, a), b - a)], fine.at[span(pick(x0 - b, x1 + a), b - a), 0:by], even - odd, 0)])
+        for a, b in steps
+    ]
+    places2 = []
+    for k in range(wy):
+        at = wide2 * k
+        places2 += [(at, ey * k - at), (at + ey + 2, ey * k - 3 - ey - at), (at + ey + 3, 1000)]
+    y_table(ty2, 2, wide2, wy * wide2, low_y * ey + 1 + radius, wy * ey if ny <= 2 * reach + 1 else 0, places2)
     z_table(tz2, 2, ez)
-
-    cols2[spot] = l2w[...]
-    arrive(fan)
-    for k in range(wy):
-        strip2[:, k * ey : (k + 1) * ey, :] = cols2[k, :, 0:ey, :]
-    for k in range(wy):
-        for at, place in ((ey, (k + 1) * ey), (ey + 1, (k + 1) * ey + 1), (ey + 2, k * ey - 1)):
-            if ny <= 2 * reach + 1:
-                place %= wy * ey
-            if 0 <= place < wy * ey:
-                strip2[:, place : place + 1, :] += cols2[k, :, at : at + 1, :]
-    tail = margin - ex + 2
-    lines = both([
-        remote(strip2, seen2.at[0], 1, 0),
-        remote(strip2, seen2.at[1], -1, 0),
-        remote(strip2.at[rows2 - tail : rows2], far2.at[0], 2, 0),
-        remote(strip2.at[0:tail], far2.at[1], -2, 0),
-    ])
-    far = both([
-        remote(q.at[bx - radius : bx], fine.at[0:x0, 0:by], 1, 0),
-        remote(q.at[0:radius], fine.at[x1 : x1 + radius, 0:by], -1, 0),
-    ])
     fine[x0:x1, 0:by, :] = q[...]
     y_table(ty0, 0, by, by + 24, radius, 0, [(by, -by - 8), (by + 8, -8), (by + 16, -by - 16 - radius), (by + 16 + extra, -8 - extra), (by + 16 + 2 * extra, 1000)])
     y_table(ty1, 1, wide1, wide1 + 2 * hy, radius + 1, 0, [(hy + 1, -hy - 2), (hy + 2, 1000), (wide1, -wide1 - hy + 1), (wide1 + hy, -wide1 - 1)])
@@ -243,6 +244,19 @@
 
     z_table(tz1, 1, hz)
 
+    arrive(lines)
+    home = radius
+    pairs = cols2.shape[1]
+    whole = [None] * (2 * pairs)
+    for first, source in ((home, l2p), (home - ex, seen2.at[0]), (home + ex, seen2.at[1]), (home - 2 * ex, seen2.at[2]), (home + 2 * ex, seen2.at[3])):
+        for r in range(rows2):
+            if 0 <= first + r < rows2 + 2 * radius:
+                piece = source[r % half2][:, (r // half2) * ez : (r // half2 + 1) * ez]
+                whole[first + r] = piece if whole[first + r] is None else whole[first + r] + piece
+    for j in range(pairs):
+        top[j] = jnp.concatenate([jnp.zeros((wide2, ez), F32) if v is None else v for v in (whole[j], whole[j + pairs])], axis=1)
+    fan = both([remote(top, cols2.at[k], 0, -(low_y + k)) for k in range(wy) if low_y + k])
+    cols2[-low_y] = top[...]
     arrive(rim)
     mid[0 : margin + 1, 0:wide1] = low1[...]
     mid[margin + 1 : margin + hx - 1, 0:wide1] = l1w[2:hx]
@@ -256,7 +270,8 @@
         remote(left1, mid.at[:, wide1 : wide1 + hy], 0, 1),
         remote(right1, mid.at[:, wide1 + hy : wide1 + 2 * hy], 0, -1),
     ])
-    outer = list(range(x0)) + list(range(x1, x1 + radius))
+    far = both([remote(q.at[span(pick(0, bx - radius), radius)], fine.at[span(pick(x1, 0), radius), 0:by], odd - even, 0)])
+
     def correlate_y(ref, source, table, rows, step, first=0):
         width = table.shape[0] // terms
 
@@ -283,10 +298,10 @@
 
         repeat(rows, step, one)
 
-    def correlate_z(ref, table, a, b):
-        size = (b - a) * ref.shape[2]
-        high = ref[0, a:b].reshape(size, ref.shape[3])
-        low = ref[1, a:b].reshape(size, ref.shape[3])
+    def correlate_z(ref, table, rows, count):
+        size = count * ref.shape[2]
+        high = ref[0, rows].reshape(size, ref.shape[3])
+        low = ref[1, rows].reshape(size, ref.shape[3])
         return dot(high, table[0]) + dot(low, table[0]) + dot(high, table[1])
 
     def prolong_x(source, j, first):
@@ -300,62 +315,81 @@
     arrive(side)
     unpack(range(x0, x1), 0)
     correlate_y(y0, fine, ty0, bx, 4, x0)
-
-    arrive(lines)
-    top[...] = jnp.zeros(top.shape, F32)
-    home = radius
-    for first, source in ((home, strip2), (home - ex, seen2.at[0]), (home + ex, seen2.at[1])):
-        top[first : first + rows2] += source[...]
-    top[0:tail] += far2[0]
-    top[home + 2 * ex : home + 2 * ex + tail] += far2[1]
-    correlate_y(y2, top, ty2, top.shape[0], top.shape[0])
+    correlate_x(s0, y0, 0, bx - 2 * radius, 0, 1, radius)
+    def pack(start, size, group):
+        for n in range(size):
+            g, r = group + n // per, extra * (n % per)
+            ext[0, g, r : r + extra] = fine[start + n, by - radius : by - 8, :]
+            ext[1, g, r : r + extra] = fine[start + n, 8:radius, :]
+        rows, groups = span(start, size), slice(group, group - (-size // per))
+        return both([
+            remote(fine.at[rows, by - 8 : by], fine.at[rows, by : by + 8], 0, 1),
+            remote(fine.at[rows, 0:8], fine.at[rows, by + 8 : by + 16], 0, -1),
+            remote(ext.at[0, groups], got.at[0, groups], 0, 1),
+            remote(ext.at[1, groups], got.at[1, groups], 0, -1),
+        ])
+
+    parts = [(0, radius, pick(0, x1), pick(0, bx - radius))] + [
+        (a, b, pick(x1 + a, x0 - b), pick(bx - radius + a, radius - b)) for a, b in steps
+    ]
+    groups = [g1]
+    for a, b, _, _ in parts:
+        groups.append(groups[-1] + -(-(b - a) // per))
+    corners = []
+
+    def relay(copies):
+        part = len(corners)
+        a, b, halo, _ = parts[part]
+        arrive(copies)
+        corners.append(pack(halo, b - a, groups[part]))
+
+    arrive(fan)
+    for j in range(pairs):
+        value = dot(ty2[...], stacked3(jnp.concatenate([cols2[k, j] for k in range(wy)], axis=0)))
+        for member in range(terms):
+            y2[member, j] = value[member * wide2 : (member + 1) * wide2, 0:ez]
+            y2[member, j + pairs] = value[member * wide2 : (member + 1) * wide2, ez : 2 * ez]
     correlate_x(s2, y2, 2, rows2, 0, 1)
-    tx[...] = correlate_z(s2, tz2, 0, rows2).reshape(tx.shape)
+    tx[...] = correlate_z(s2, tz2, slice(0, rows2), rows2).reshape(tx.shape)
     for j in range(hx + 2):
         ty[j] = dot(uy2[...], stacked2(prolong_x(tx, j - 1, -1)))
     high, low = halves(ty[...].reshape((hx + 2) * ty.shape[1], ez))
     lifted = dot(high, uz2[...]) + dot(low, uz2[...])
 
     md[...] = lifted.reshape(md.shape)
+    relay(far)
     arrive(rim2)
-    correlate_y(y1, mid, ty1, hx + 2 * margin, 2)
+    correlate_y(y1, mid, ty1, hx + 2 * margin, (hx + 2 * margin) // 2)
     correlate_x(s1, y1, 1, hx + 2, 0, 1)
-    md[...] += correlate_z(s1, tz1, 0, hx + 2).reshape(md.shape)
+    md[...] += correlate_z(s1, tz1, slice(0, hx + 2), hx + 2).reshape(md.shape)
     for j in range(bx):
         high, low = halves(dot(uy1[...], stacked2(prolong_x(md, j, -1))))
         my[0, j] = high
         my[1, j] = low
 
-    def finish(a, b):
-        high = my[0, a:b].reshape((b - a) * by, hz)
-        low = my[1, a:b].reshape((b - a) * by, hz)
-        total = correlate_z(s0, tz0, a, b) + dot(high, uz1[...]) + dot(low, uz1[...])
-        out[a:b] = total.reshape(b - a, by, bz)
-
-    correlate_x(s0, y0, 0, bx - 2 * radius, 0, 1, radius)
-    finish(radius, bx - radius)
-    arrive(far)
-    for n, i in enumerate(outer):
-        g, r = g1 + n // per, extra * (n % per)
-        ext[0, g, r : r + extra] = fine[i, by - radius : by - 8, :]
-        ext[1, g, r : r + extra] = fine[i, 8:radius, :]
-    g2 = ext.shape[1]
-    corner = both(
-        [remote(fine.at[a:b, by - 8 : by], fine.at[a:b, by : by + 8], 0, 1) for a, b in ((0, x0), (x1, x1 + radius))]
-        + [remote(fine.at[a:b, 0:8], fine.at[a:b, by + 8 : by + 16], 0, -1) for a, b in ((0, x0), (x1, x1 + radius))]
-        + [remote(ext.at[0, g1:g2], got.at[0, g1:g2], 0, 1), remote(ext.at[1, g1:g2], got.at[1, g1:g2], 0, -1)]
-    )
-
-    arrive(corner)
-    unpack(outer, g1)
-    correlate_y(y0, fine, ty0, x0, 5)
-    correlate_y(y0, fine, ty0, radius, 5, x1)
-    correlate_x(s0, y0, 0, radius, 0, 1)
-    correlate_x(s0, y0, 0, radius, 0, 1, bx - radius)
-    finish(0, radius)
-    finish(bx - radius, bx)
-    for copy in fan + rim + side + lines + far + rim2 + corner:
+    def finish(start, size):
+        rows = span(start, size)
+        high = my[0, rows].reshape(size * by, hz)
+        low = my[1, rows].reshape(size * by, hz)
+        total = correlate_z(s0, tz0, rows, size) + dot(high, uz1[...]) + dot(low, uz1[...])
+        out[rows] = total.reshape(size, by, bz)
+
+    for copies in near:
+        relay(copies)
+    finish(radius, bx - 2 * radius)
+    for part, (a, b, halo, target) in enumerate(parts):
+        arrive(corners[part])
+        unpack([halo + n for n in range(b - a)], groups[part])
+        correlate_y(y0, fine, ty0, b - a, 2, halo)
+        correlate_x(s0, y0, 0, b - a, 0, 1, target)
+        finish(target, b - a)
+    for copy in fan + rim + side + lines + sum(near, []) + far + rim2 + sum(corners, []):
         copy.wait_send()
+
+
+def near_steps(radius):
+    first = min(radius, radius // 2 + radius // 2 % 2)
+    return [(0, first), (first, radius)]
 
 
 def cyclic_restrict(n):
@@ -386,11 +420,12 @@
     wide2 = ey + 8
     uy2 = lifted_table(list(range(-1, hy + 1)), list(range(-1, ey + 2)) + [None] * (wide2 - ey - 3), wide1)
     uy1 = lifted_table(list(range(by)), list(range(-1, hy + 1)) + [None] * (wide1 - hy - 2), by)
-    fixed = [twice(ry1), jnp.asarray(rz1, BF16), twice(ry2), jnp.asarray(rz2, BF16), twice(uy2),
+    fixed = [twice(ry1), jnp.asarray(rz1, BF16), twice(ry2), jnp.asarray(np.kron(np.eye(2), rz2), BF16), twice(uy2),
              jnp.asarray(rz2.T, BF16), twice(uy1), jnp.asarray(rz1.T, BF16)]
     rows1, rows2 = hx + 2, ex + 3
+    half2, pairs = (rows2 + 1) // 2, (rows2 + 2 * radius + 1) // 2
     extra = radius - 8
-    packed = -(-(bx + 2 * radius) * extra // 8)
+    packed = bx * extra // 8 + sum(-(-(b - a) * extra // 8) for a, b in near_steps(radius) + [(0, radius)])
     scratch = [
         pltpu.VMEM(shape, dtype)
         for shape, dtype in (
@@ -402,15 +437,13 @@
             ((hx + 2 * margin, hy, hz), F32),
             ((margin + 1, wide1, hz), F32),
             ((margin + 1, wide1, hz), F32),
-            ((rows2, wide2, ez), F32),
-            ((wy, rows2, wide2, ez), F32),
-            ((2, rows2, wy * ey, ez), F32),
-            ((rows2, wy * ey, ez), F32),
-            ((2, margin - ex + 2, wy * ey, ez), F32),
-            ((rows2 + 2 * radius, wy * ey, ez), F32),
+            ((half2, wide2, 2 * ez), F32),
+            ((wy, pairs, wide2, 2 * ez), F32),
+            ((4, half2, wide2, 2 * ez), F32),
+            ((pairs, wide2, 2 * ez), F32),
             ((terms * by, 3 * (by + 24)), BF16),
             ((terms * wide1, 3 * (wide1 + 2 * hy)), BF16),
-            ((terms * wide2, 3 * wy * ey), BF16),
+            ((terms * wide2, 3 * wy * wide2), BF16),
             ((2, terms * bz, bz), BF16),
             ((2, terms * hz, hz), BF16),
             ((2, terms * ez, ez), BF16),
@@ -418,11 +451,11 @@
             ((2, bx, by, terms * bz), BF16),
             ((terms, hx + 2 * margin, wide1, hz), F32),
             ((2, hx + 2, wide1, terms * hz), BF16),
-            ((terms, rows2 + 2 * radius, wide2, ez), F32),
+            ((terms, 2 * pairs, wide2, ez), F32),
             ((2, rows2, wide2, terms * ez), BF16),
             ((rows1, wide1, bz), F32),
             ((rows1, wide1, hz), F32),
-            ((rows2, wide2, hz), F32),
+            ((2 * half2, wide2, hz), F32),
             ((rows2, wide2, ez), F32),
             ((hx + 2, wide1, ez), F32),
             ((hx + 2, wide1, hz), F32),

time: 55.2 us -> 44.5 us (0.81)
  Pallas kernels: 52.7 us -> 42 us
    pallas_call x1, Pallas kernels: 52.7 us -> 42 us  [body(): pl.pallas_call(functools.partial(kernel, nx, ny, radius, terms), out_shap...]
where the time goes in v1:
time: 44.5 us; the launch traced here: 44.4 us
  Pallas kernels  42 us (94%)
  local copies, waits for them, and re-layouts  2.31 us (5%)
    pallas_call x1, Pallas kernels, body(): pl.pallas_call(functools.partial(kernel, nx, ny, radius, terms), out_shap...  42 us
    unnamed x1, local copies, waits for them, and re-layouts  2.31 us

profile of v1, /device:TPU:1, one launch (start us, length us, event | category | flops | bytes accessed | tf_op | source)
XLA Modules:
  0.0 44.4 jit_solution(6484173325768848869)
XLA Ops:
  0.0 42.0 %shard_map.100 = f32[32,32,256]{2,1,0:T(8,128)} custom-call(f32[3,3,21]{2,1,0:T(4,128)} %taps.1, f32[32,32,256]{2,1,0:T(8,128)} %q.1, bf16[24,64]{1,0:T(8,128)(2,1)} %constant.16.clone.ry1, bf16[256,128]{1,0:T(8,128)(2,1)} %constant.17.clone.rz1, bf16[16,48]{1,0:T(8,128)(2,1)} %constant.18.clone.ry2, bf16[256,128]{1,0:T(8,128)(2,1)} %constant.19.clone.rz2, ...), custom_call_target="tpu_custom_call" | custom-call | tf_op jit(solution)/shard_map/pallas_call | solution.py:468
  42.1 2.3 %copy.12 = f32[32,32,256]{2,1,0:T(8,128)} copy(f32[32,32,256]{2,1,0:T(8,128)} %shard_map.100) | data formatting | bytes 2097152

commit v2 on v1

--- a/solution.py
+++ b/solution.py
@@ -68,11 +68,14 @@
     lax.fori_loop(0, count // step, trip, 0)
 
 
-def kernel(nx, ny, radius, terms, taps, q, ry1, rz1, ry2, rz2, uy2, uz2, uy1, uz1, out,
-           fine, mid, ext, got, left1, right1, low1, high1, l2p, cols2, seen2, top,
+def kernel(nx, ny, radius, terms, *refs):
+    given, out, held, refs = refs[:10], refs[10], refs[11:20], refs[20:]
+    taps, ry1, rz1, ry2, rz2, uy2, uz2, uy1, uz1 = held
+    (fine, mid, ext, got, left1, right1, low1, high1, l2p, cols2, seen2, top,
            ty0, ty1, ty2, tz0, tz1, tz2, y0, s0, y1, s1, y2, s2, r1, l1w, l2y, tx, ty, md, my,
-           send, recv):
-    bx, by, bz = q.shape
+     edge, edge_in, stage, send, recv, load, store) = refs
+    bx, by, bz = given[1].shape
+    x0, x1 = radius, radius + bx
     hx, hy, hz = bx // 2, by // 2, bz // 2
     ex, ey, ez = bx // 4, by // 4, bz // 4
     count = 2 * radius + 1
@@ -96,6 +99,13 @@
     barrier = pltpu.get_barrier_semaphore()
     for dx, dy in peers.values():
         pl.semaphore_signal(barrier, inc=1, device_id=device(dx, dy), device_id_type=MESH)
+
+    fetched = [
+        pltpu.make_async_copy(source, target, load.at[n])
+        for n, (source, target) in enumerate(zip(given, [taps, fine.at[x0:x1, 0:by]] + list(held[1:])))
+    ]
+    for copy in fetched:
+        copy.start()
 
     def tap(level, member, position):
         return taps[level, member, position]
@@ -162,7 +172,6 @@
         for copy in copies:
             copy.wait_recv()
 
-    x0, x1 = radius, radius + bx
     extra = radius - 8
     per = 8 // extra
     def weighted(source, i, low, high):
@@ -173,11 +182,13 @@
                 total = piece if total is None else total + piece
         return total
 
+    for copy in fetched:
+        copy.wait()
     rows1, rows2 = hx + 2, ex + 3
     half2 = l2p.shape[0]
     wide1, wide2 = ry1.shape[0], ry2.shape[0]
     for i in range(rows1):
-        r1[i] = dot(ry1[...], stacked2(weighted(lambda f: q[f], i - 1, 0, bx)))
+        r1[i] = dot(ry1[...], stacked2(weighted(lambda f: fine[x0 + f, 0:by], i - 1, 0, bx)))
     high, low = halves(r1[...].reshape(rows1 * wide1, bz))
     l1w[...] = (dot(high, rz1[...]) + dot(low, rz1[...])).reshape(rows1, wide1, hz)
     for i in range(rows2):
@@ -187,27 +198,34 @@
     high, low = halves(jnp.concatenate([l2y[0:half2], l2y[half2 : 2 * half2]], axis=2).reshape(half2 * wide2, 2 * hz))
     l2p[...] = (dot(high, rz2[...]) + dot(low, rz2[...])).reshape(l2p.shape)
     pl.semaphore_wait(barrier, len(peers))
-    spot = -low_y
     lines = both([
         remote(l2p, seen2.at[0], 1, 0),
         remote(l2p, seen2.at[1], -1, 0),
         remote(l2p, seen2.at[2], 2, 0),
         remote(l2p, seen2.at[3], -2, 0),
     ])
-    rim = both([
-        remote(l1w.at[rows1 - margin - 1 : rows1], low1, 1, 0),
-        remote(l1w.at[0 : margin + 1], high1, -1, 0),
-    ])
+    def edge_at(ref, d, i):
+        return ref.at[d, i // 4, 2 * (i % 4) : 2 * (i % 4) + 2]
+
+    first1 = (rows1 - margin - 1, 0)
+    rim = []
+    for d, dx in ((0, 1), (1, -1)):
+        rim.append(remote(l1w.at[first1[d] : first1[d] + margin + 1, 0:hy], (low1, high1)[d], dx, 0))
+        rim[-1].start()
+    for i in range(margin + 1):
+        for d in range(2):
+            edge_at(edge, d, i)[...] = l1w[first1[d] + i, hy : hy + 2]
+    rim += both([remote(edge.at[d], edge_in.at[d], dx, 0) for d, dx in ((0, 1), (1, -1))])
     g1 = bx // per
     steps = near_steps(radius)
     side = both([
-        remote(q.at[:, by - 8 : by], fine.at[x0:x1, by : by + 8], 0, 1),
-        remote(q.at[:, 0:8], fine.at[x0:x1, by + 8 : by + 16], 0, -1),
+        remote(fine.at[x0:x1, by - 8 : by], fine.at[x0:x1, by : by + 8], 0, 1),
+        remote(fine.at[x0:x1, 0:8], fine.at[x0:x1, by + 8 : by + 16], 0, -1),
     ])
     for i in range(bx):
         g, r = i // per, extra * (i % per)
-        ext[0, g, r : r + extra] = q[i, by - radius : by - 8]
-        ext[1, g, r : r + extra] = q[i, 8:radius]
+        ext[0, g, r : r + extra] = fine[x0 + i, by - radius : by - 8]
+        ext[1, g, r : r + extra] = fine[x0 + i, 8:radius]
 
     side += both([
         remote(ext.at[0, 0:g1], got.at[0, 0:g1], 0, 1),
@@ -220,7 +238,7 @@
         return pl.ds(start, size)
 
     near = [
-        both([remote(q.at[span(pick(bx - b, a), b - a)], fine.at[span(pick(x0 - b, x1 + a), b - a), 0:by], even - odd, 0)])
+        both([remote(fine.at[span(pick(x1 - b, x0 + a), b - a), 0:by], fine.at[span(pick(x0 - b, x1 + a), b - a), 0:by], even - odd, 0)])
         for a, b in steps
     ]
     places2 = []
@@ -229,7 +247,6 @@
         places2 += [(at, ey * k - at), (at + ey + 2, ey * k - 3 - ey - at), (at + ey + 3, 1000)]
     y_table(ty2, 2, wide2, wy * wide2, low_y * ey + 1 + radius, wy * ey if ny <= 2 * reach + 1 else 0, places2)
     z_table(tz2, 2, ez)
-    fine[x0:x1, 0:by, :] = q[...]
     y_table(ty0, 0, by, by + 24, radius, 0, [(by, -by - 8), (by + 8, -8), (by + 16, -by - 16 - radius), (by + 16 + extra, -8 - extra), (by + 16 + 2 * extra, 1000)])
     y_table(ty1, 1, wide1, wide1 + 2 * hy, radius + 1, 0, [(hy + 1, -hy - 2), (hy + 2, 1000), (wide1, -wide1 - hy + 1), (wide1 + hy, -wide1 - 1)])
     z_table(tz0, 0, bz)
@@ -255,23 +272,12 @@
                 whole[first + r] = piece if whole[first + r] is None else whole[first + r] + piece
     for j in range(pairs):
         top[j] = jnp.concatenate([jnp.zeros((wide2, ez), F32) if v is None else v for v in (whole[j], whole[j + pairs])], axis=1)
-    fan = both([remote(top, cols2.at[k], 0, -(low_y + k)) for k in range(wy) if low_y + k])
+    if ny == 4:
+        turn = 1 - 2 * lax.rem(me_y, 2)
+        fan = both([remote(top, cols2.at[3], 0, 2), remote(top, cols2.at[1 - turn], 0, turn)])
+    else:
+        fan = both([remote(top, cols2.at[k], 0, -(low_y + k)) for k in range(wy) if low_y + k])
     cols2[-low_y] = top[...]
-    arrive(rim)
-    mid[0 : margin + 1, 0:wide1] = low1[...]
-    mid[margin + 1 : margin + hx - 1, 0:wide1] = l1w[2:hx]
-    mid[margin + hx - 1 : margin + hx + margin, 0:wide1] = high1[...]
-    for i, j in ((margin - 1, 0), (margin, 1), (margin + hx - 1, hx), (margin + hx, hx + 1)):
-        mid[i, 0:wide1] += l1w[j]
-    left1[...] = mid[:, 1 : hy + 1, :]
-    right1[:, 0:1, :] = mid[:, hy + 1 : hy + 2, :]
-    right1[:, 1:hy, :] = mid[:, 0 : hy - 1, :]
-    rim2 = both([
-        remote(left1, mid.at[:, wide1 : wide1 + hy], 0, 1),
-        remote(right1, mid.at[:, wide1 + hy : wide1 + 2 * hy], 0, -1),
-    ])
-    far = both([remote(q.at[span(pick(0, bx - radius), radius)], fine.at[span(pick(x1, 0), radius), 0:by], odd - even, 0)])
-
     def correlate_y(ref, source, table, rows, step, first=0):
         width = table.shape[0] // terms
 
@@ -298,6 +304,28 @@
 
         repeat(rows, step, one)
 
+    mid[:, hy:wide1] = jnp.zeros((mid.shape[0], wide1 - hy, hz), F32)
+    arrive(side)
+    unpack(range(x0, x1), 0)
+    correlate_y(y0, fine, ty0, bx, 4, x0)
+    mid[margin + 1 : margin + hx - 1, 0:wide1] = l1w[2:hx]
+    arrive(rim)
+    mid[0 : margin + 1, 0:hy] = low1[...]
+    mid[margin + hx - 1 : margin + hx + margin, 0:hy] = high1[...]
+    for i in range(margin + 1):
+        for d, at in ((0, 0), (1, margin + hx - 1)):
+            mid[at + i, hy : hy + 2] = edge_at(edge_in, d, i)[...]
+    for i, j in ((margin - 1, 0), (margin, 1), (margin + hx - 1, hx), (margin + hx, hx + 1)):
+        mid[i, 0:wide1] += l1w[j]
+    left1[...] = mid[:, 1 : hy + 1, :]
+    right1[:, 0:1, :] = mid[:, hy + 1 : hy + 2, :]
+    right1[:, 1:hy, :] = mid[:, 0 : hy - 1, :]
+    rim2 = both([
+        remote(left1, mid.at[:, wide1 : wide1 + hy], 0, 1),
+        remote(right1, mid.at[:, wide1 + hy : wide1 + 2 * hy], 0, -1),
+    ])
+    far = both([remote(fine.at[span(pick(x0, x1 - radius), radius), 0:by], fine.at[span(pick(x1, 0), radius), 0:by], odd - even, 0)])
+
     def correlate_z(ref, table, rows, count):
         size = count * ref.shape[2]
         high = ref[0, rows].reshape(size, ref.shape[3])
@@ -312,9 +340,6 @@
         c = (j - 1) // 2 - first
         return source[c] * 0.5 + source[c + 1] * 0.5
 
-    arrive(side)
-    unpack(range(x0, x1), 0)
-    correlate_y(y0, fine, ty0, bx, 4, x0)
     correlate_x(s0, y0, 0, bx - 2 * radius, 0, 1, radius)
     def pack(start, size, group):
         for n in range(size):
@@ -343,7 +368,12 @@
         arrive(copies)
         corners.append(pack(halo, b - a, groups[part]))
 
-    arrive(fan)
+    if ny == 4:
+        arrive(fan[:1])
+        fan += both([remote(cols2.at[3], cols2.at[1 + turn], 0, turn)])
+        arrive(fan[1:])
+    else:
+        arrive(fan)
     for j in range(pairs):
         value = dot(ty2[...], stacked3(jnp.concatenate([cols2[k, j] for k in range(wy)], axis=0)))
         for member in range(terms):
@@ -357,22 +387,26 @@
     lifted = dot(high, uz2[...]) + dot(low, uz2[...])
 
     md[...] = lifted.reshape(md.shape)
-    relay(far)
     arrive(rim2)
     correlate_y(y1, mid, ty1, hx + 2 * margin, (hx + 2 * margin) // 2)
     correlate_x(s1, y1, 1, hx + 2, 0, 1)
+    relay(far)
     md[...] += correlate_z(s1, tz1, slice(0, hx + 2), hx + 2).reshape(md.shape)
     for j in range(bx):
         high, low = halves(dot(uy1[...], stacked2(prolong_x(md, j, -1))))
         my[0, j] = high
         my[1, j] = low
 
+    stored = []
+
     def finish(start, size):
         rows = span(start, size)
         high = my[0, rows].reshape(size * by, hz)
         low = my[1, rows].reshape(size * by, hz)
         total = correlate_z(s0, tz0, rows, size) + dot(high, uz1[...]) + dot(low, uz1[...])
-        out[rows] = total.reshape(size, by, bz)
+        stage[rows] = total.reshape(size, by, bz)
+        stored.append(pltpu.make_async_copy(stage.at[rows], out.at[rows], store.at[len(stored)]))
+        stored[-1].start()
 
     for copies in near:
         relay(copies)
@@ -383,6 +417,8 @@
         correlate_y(y0, fine, ty0, b - a, 2, halo)
         correlate_x(s0, y0, 0, b - a, 0, 1, target)
         finish(target, b - a)
+    for copy in stored:
+        copy.wait()
     for copy in fan + rim + side + lines + sum(near, []) + far + rim2 + sum(corners, []):
         copy.wait_send()
 
@@ -390,6 +426,19 @@
 def near_steps(radius):
     first = min(radius, radius // 2 + radius // 2 % 2)
     return [(0, first), (first, radius)]
+
+
+def hand_over(pieces, source, target, held, load, store):
+    size = source.shape[0] // pieces
+    reads = [pltpu.make_async_copy(source.at[i * size : (i + 1) * size], held.at[i * size : (i + 1) * size], load.at[i]) for i in range(pieces)]
+    writes = [pltpu.make_async_copy(held.at[i * size : (i + 1) * size], target.at[i * size : (i + 1) * size], store.at[i]) for i in range(pieces)]
+    for copy in reads:
+        copy.start()
+    for before, after in zip(reads, writes):
+        before.wait()
+        after.start()
+    for copy in writes:
+        copy.wait()
 
 
 def cyclic_restrict(n):
@@ -426,7 +475,7 @@
     half2, pairs = (rows2 + 1) // 2, (rows2 + 2 * radius + 1) // 2
     extra = radius - 8
     packed = bx * extra // 8 + sum(-(-(b - a) * extra // 8) for a, b in near_steps(radius) + [(0, radius)])
-    scratch = [
+    scratch = [pltpu.SMEM(kernel_taps.shape, F32)] + [pltpu.VMEM(table.shape, table.dtype) for table in fixed] + [
         pltpu.VMEM(shape, dtype)
         for shape, dtype in (
             ((bx + 2 * radius, by + 24, bz), F32),
@@ -435,8 +484,8 @@
             ((2, packed, 8, bz), F32),
             ((hx + 2 * margin, hy, hz), F32),
             ((hx + 2 * margin, hy, hz), F32),
-            ((margin + 1, wide1, hz), F32),
-            ((margin + 1, wide1, hz), F32),
+            ((margin + 1, hy, hz), F32),
+            ((margin + 1, hy, hz), F32),
             ((half2, wide2, 2 * ez), F32),
             ((wy, pairs, wide2, 2 * ez), F32),
             ((4, half2, wide2, 2 * ez), F32),
@@ -460,21 +509,39 @@
             ((hx + 2, wide1, ez), F32),
             ((hx + 2, wide1, hz), F32),
             ((2, bx, by, hz), BF16),
+            ((2, -(-2 * (margin + 1) // 8), 8, hz), F32),
+            ((2, -(-2 * (margin + 1) // 8), 8, hz), F32),
+            (charges.shape, F32),
         )
     ] + [
         pltpu.SemaphoreType.DMA((48,)),
         pltpu.SemaphoreType.DMA((48,)),
+        pltpu.SemaphoreType.DMA((2 + len(fixed),)),
+        pltpu.SemaphoreType.DMA((8,)),
     ]
-    return pl.pallas_call(
+    result = pl.pallas_call(
         functools.partial(kernel, nx, ny, radius, terms),
         out_shape=jax.ShapeDtypeStruct(charges.shape, F32),
-        in_specs=[pl.BlockSpec(memory_space=pltpu.SMEM)] + [pl.BlockSpec(memory_space=pltpu.VMEM)] * 9,
-        out_specs=pl.BlockSpec(memory_space=pltpu.VMEM),
+        in_specs=[pl.BlockSpec(memory_space=pltpu.HBM)] * (2 + len(fixed)),
+        out_specs=pl.BlockSpec(memory_space=pltpu.HBM),
         scratch_shapes=scratch,
         compiler_params=pltpu.CompilerParams(
             collective_id=0, has_side_effects=True, vmem_limit_bytes=60 * 2**20
         ),
     )(kernel_taps, charges, *fixed)
+    pieces = 8
+    return pl.pallas_call(
+        functools.partial(hand_over, pieces),
+        out_shape=jax.ShapeDtypeStruct(charges.shape, F32),
+        in_specs=[pl.BlockSpec(memory_space=pltpu.HBM)],
+        out_specs=pl.BlockSpec(memory_space=pltpu.HBM),
+        scratch_shapes=[
+            pltpu.VMEM(charges.shape, F32),
+            pltpu.SemaphoreType.DMA((pieces,)),
+            pltpu.SemaphoreType.DMA((pieces,)),
+        ],
+        compiler_params=pltpu.CompilerParams(vmem_limit_bytes=60 * 2**20),
+    )(result)
 
 
 def solution(mesh):

time: 44.5 us -> 41.5 us (0.933)
  local copies, waits for them, and re-layouts: 2.31 us -> 0 us
  Pallas kernels: 42 us -> 41.3 us
    pallas_call x1, Pallas kernels: 42 us -> 39.2 us  [body(): pl.pallas_call(functools.partial(kernel, nx, ny, radius, terms), out_shap...]
    unnamed x1 -> x0, local copies, waits for them, and re-layouts: 2.31 us -> none
    pallas_call x0 -> x1, Pallas kernels: none -> 2.09 us  [body(): pl.pallas_call(functools.partial(hand_over, pieces), out_shape=jax.ShapeD...]
where the time goes in v2:
time: 41.5 us; the launch traced here: 41.3 us
  Pallas kernels  41.3 us (100%)
    pallas_call x1, Pallas kernels, body(): pl.pallas_call(functools.partial(kernel, nx, ny, radius, terms), out_shap...  39.2 us
    pallas_call x1, Pallas kernels, body(): pl.pallas_call(functools.partial(hand_over, pieces), out_shape=jax.ShapeD...  2.09 us

profile of v2, /device:TPU:1, one launch (start us, length us, event | category | flops | bytes accessed | tf_op | source)
XLA Modules:
  0.0 41.3 jit_solution(5455338934422441578)
XLA Ops:
  0.0 39.2 %shard_map.100.source = f32[32,32,256]{2,1,0:T(8,128)} custom-call(f32[3,3,21]{2,1,0:T(4,128)} %refs_0_.1, f32[32,32,256]{2,1,0:T(8,128)} %refs_1_.1, bf16[24,64]{1,0:T(8,128)(2,1)} %constant.16.clone.refs_2_, bf16[256,128]{1,0:T(8,128)(2,1)} %constant.17.clone.refs_3_, bf16[16,48]{1,0:T(8,128)(2,1)} %constant.18.clone.refs_4_, ...), custom_call_target="tpu_custom_call" | custom-call | tf_op jit(solution)/shard_map/pallas_call | solution.py:522
  39.3 2.1 %shard_map.101 = f32[32,32,256]{2,1,0:T(8,128)} custom-call(f32[32,32,256]{2,1,0:T(8,128)} %shard_map.100.source), custom_call_target="tpu_custom_call" | custom-call | tf_op jit(solution)/shard_map/pallas_call | solution.py:533

commit v3 on v2

--- a/solution.py
+++ b/solution.py
@@ -71,9 +71,9 @@
 def kernel(nx, ny, radius, terms, *refs):
     given, out, held, refs = refs[:10], refs[10], refs[11:20], refs[20:]
     taps, ry1, rz1, ry2, rz2, uy2, uz2, uy1, uz1 = held
-    (fine, mid, ext, got, left1, right1, low1, high1, l2p, cols2, seen2, top,
+    (fine, mid, ext, got, tips, tips_in, low1, high1, l2p, cols2, seen2, top,
            ty0, ty1, ty2, tz0, tz1, tz2, y0, s0, y1, s1, y2, s2, r1, l1w, l2y, tx, ty, md, my,
-     edge, edge_in, stage, send, recv, load, store) = refs
+     edge, edge_in, stage, part, send, recv, load, store) = refs
     bx, by, bz = given[1].shape
     x0, x1 = radius, radius + bx
     hx, hy, hz = bx // 2, by // 2, bz // 2
@@ -174,6 +174,8 @@
 
     extra = radius - 8
     per = 8 // extra
+    tip = margin - 7
+    tip_per = 8 // tip
     def weighted(source, i, low, high):
         total = None
         for k in range(-2, 3):
@@ -248,7 +250,11 @@
     y_table(ty2, 2, wide2, wy * wide2, low_y * ey + 1 + radius, wy * ey if ny <= 2 * reach + 1 else 0, places2)
     z_table(tz2, 2, ez)
     y_table(ty0, 0, by, by + 24, radius, 0, [(by, -by - 8), (by + 8, -8), (by + 16, -by - 16 - radius), (by + 16 + extra, -8 - extra), (by + 16 + 2 * extra, 1000)])
-    y_table(ty1, 1, wide1, wide1 + 2 * hy, radius + 1, 0, [(hy + 1, -hy - 2), (hy + 2, 1000), (wide1, -wide1 - hy + 1), (wide1 + hy, -wide1 - 1)])
+    low, high = wide1 + 16, wide1 + 16 + tip
+    y_table(ty1, 1, wide1, wide1 + 16 + 2 * tip, radius + 1, 0, [
+        (hy + 1, -hy - 2), (hy + 2, 1000), (wide1, -8 - wide1), (wide1 + 8, hy - wide1 - 8), (low, -margin - low),
+        (low + tip - 1, -low - tip + 1), (high, hy + 8 - high), (high + tip - 1, hy - high - tip),
+    ])
     z_table(tz0, 0, bz)
     spare = jnp.zeros((8 - 2 * extra, bz), F32)
 
@@ -305,9 +311,6 @@
         repeat(rows, step, one)
 
     mid[:, hy:wide1] = jnp.zeros((mid.shape[0], wide1 - hy, hz), F32)
-    arrive(side)
-    unpack(range(x0, x1), 0)
-    correlate_y(y0, fine, ty0, bx, 4, x0)
     mid[margin + 1 : margin + hx - 1, 0:wide1] = l1w[2:hx]
     arrive(rim)
     mid[0 : margin + 1, 0:hy] = low1[...]
@@ -317,13 +320,16 @@
             mid[at + i, hy : hy + 2] = edge_at(edge_in, d, i)[...]
     for i, j in ((margin - 1, 0), (margin, 1), (margin + hx - 1, hx), (margin + hx, hx + 1)):
         mid[i, 0:wide1] += l1w[j]
-    left1[...] = mid[:, 1 : hy + 1, :]
-    right1[:, 0:1, :] = mid[:, hy + 1 : hy + 2, :]
-    right1[:, 1:hy, :] = mid[:, 0 : hy - 1, :]
     rim2 = both([
-        remote(left1, mid.at[:, wide1 : wide1 + hy], 0, 1),
-        remote(right1, mid.at[:, wide1 + hy : wide1 + 2 * hy], 0, -1),
+        remote(mid.at[:, hy - 8 : hy], mid.at[:, wide1 : wide1 + 8], 0, 1),
+        remote(mid.at[:, 0:8], mid.at[:, wide1 + 8 : wide1 + 16], 0, -1),
     ])
+    for i in range(mid.shape[0]):
+        g, r = i // tip_per, tip * (i % tip_per)
+        for d, (a, b) in enumerate(((hy - margin, hy - 8), (8, margin))):
+            tips[d, g, r : r + tip - 1] = mid[i, a:b]
+            tips[d, g, r + tip - 1 : r + tip] = mid[i, hy + d : hy + d + 1]
+    rim2 += both([remote(tips.at[d], tips_in.at[d], 0, dy) for d, dy in ((0, 1), (1, -1))])
     far = both([remote(fine.at[span(pick(x0, x1 - radius), radius), 0:by], fine.at[span(pick(x1, 0), radius), 0:by], odd - even, 0)])
 
     def correlate_z(ref, table, rows, count):
@@ -340,7 +346,41 @@
         c = (j - 1) // 2 - first
         return source[c] * 0.5 + source[c + 1] * 0.5
 
+    arrive(side)
+    unpack(range(x0, x1), 0)
+    correlate_y(y0, fine, ty0, bx, 4, x0)
     correlate_x(s0, y0, 0, bx - 2 * radius, 0, 1, radius)
+    if ny == 4:
+        arrive(fan[:1])
+        fan = both([remote(cols2.at[3], cols2.at[1 + turn], 0, turn)]) + fan[1:] + fan[:1]
+    for e in range(radius):
+        for edge_of, i in ((0, e), (1, bx - 1 - e)):
+            for member in range(terms):
+                total = None
+                for position in range(count):
+                    if x0 <= i + position < x1:
+                        piece = y0[member, i + position] * tap(0, member, position)
+                        total = piece if total is None else total + piece
+                part[edge_of, e, member] = total
+
+    def add_halo(edge_of, a, b):
+        def choose(first, last):
+            return (1 - edge_of) * first + edge_of * last
+
+        for e in range(radius - a):
+            i = choose(e, bx - 1 - e)
+            for member in range(terms):
+                total = part[edge_of, e, member]
+                for k in range(a, min(b, radius - e)):
+                    weight = tap(0, member, choose(radius - 1 - k - e, radius + 1 + k + e))
+                    total = total + y0[member, choose(x0 - 1 - k, x1 + k)] * weight
+                if radius - e > b:
+                    part[edge_of, e, member] = total
+                else:
+                    high, low = halves(total)
+                    s0[0, i, :, member * bz : (member + 1) * bz] = high
+                    s0[1, i, :, member * bz : (member + 1) * bz] = low
+
     def pack(start, size, group):
         for n in range(size):
             g, r = group + n // per, extra * (n % per)
@@ -363,17 +403,12 @@
     corners = []
 
     def relay(copies):
-        part = len(corners)
-        a, b, halo, _ = parts[part]
+        n = len(corners)
+        a, b, halo, _ = parts[n]
         arrive(copies)
-        corners.append(pack(halo, b - a, groups[part]))
-
-    if ny == 4:
-        arrive(fan[:1])
-        fan += both([remote(cols2.at[3], cols2.at[1 + turn], 0, turn)])
-        arrive(fan[1:])
-    else:
-        arrive(fan)
+        corners.append(pack(halo, b - a, groups[n]))
+
+    arrive(fan[:2] if ny == 4 else fan)
     for j in range(pairs):
         value = dot(ty2[...], stacked3(jnp.concatenate([cols2[k, j] for k in range(wy)], axis=0)))
         for member in range(terms):
@@ -388,6 +423,10 @@
 
     md[...] = lifted.reshape(md.shape)
     arrive(rim2)
+    for i in range(mid.shape[0]):
+        g, r = i // tip_per, tip * (i % tip_per)
+        for d in range(2):
+            mid[i, wide1 + 16 + tip * d : wide1 + 16 + tip * (d + 1)] = tips_in[d, g, r : r + tip]
     correlate_y(y1, mid, ty1, hx + 2 * margin, (hx + 2 * margin) // 2)
     correlate_x(s1, y1, 1, hx + 2, 0, 1)
     relay(far)
@@ -411,11 +450,11 @@
     for copies in near:
         relay(copies)
     finish(radius, bx - 2 * radius)
-    for part, (a, b, halo, target) in enumerate(parts):
-        arrive(corners[part])
-        unpack([halo + n for n in range(b - a)], groups[part])
-        correlate_y(y0, fine, ty0, b - a, 2, halo)
-        correlate_x(s0, y0, 0, b - a, 0, 1, target)
+    for n, (a, b, halo, target) in enumerate(parts):
+        arrive(corners[n])
+        unpack([halo + k for k in range(b - a)], groups[n])
+        correlate_y(y0, fine, ty0, b - a, (b - a) // 2, halo)
+        add_halo(even if n else odd, a, b)
         finish(target, b - a)
     for copy in stored:
         copy.wait()
@@ -474,16 +513,17 @@
     rows1, rows2 = hx + 2, ex + 3
     half2, pairs = (rows2 + 1) // 2, (rows2 + 2 * radius + 1) // 2
     extra = radius - 8
+    tip = margin - 7
     packed = bx * extra // 8 + sum(-(-(b - a) * extra // 8) for a, b in near_steps(radius) + [(0, radius)])
     scratch = [pltpu.SMEM(kernel_taps.shape, F32)] + [pltpu.VMEM(table.shape, table.dtype) for table in fixed] + [
         pltpu.VMEM(shape, dtype)
         for shape, dtype in (
             ((bx + 2 * radius, by + 24, bz), F32),
-            ((hx + 2 * margin, wide1 + 2 * hy, hz), F32),
+            ((hx + 2 * margin, wide1 + 16 + 2 * tip, hz), F32),
             ((2, packed, 8, bz), F32),
             ((2, packed, 8, bz), F32),
-            ((hx + 2 * margin, hy, hz), F32),
-            ((hx + 2 * margin, hy, hz), F32),
+            ((2, -(-(hx + 2 * margin) // (8 // tip)), 8, hz), F32),
+            ((2, -(-(hx + 2 * margin) // (8 // tip)), 8, hz), F32),
             ((margin + 1, hy, hz), F32),
             ((margin + 1, hy, hz), F32),
             ((half2, wide2, 2 * ez), F32),
@@ -491,7 +531,7 @@
             ((4, half2, wide2, 2 * ez), F32),
             ((pairs, wide2, 2 * ez), F32),
             ((terms * by, 3 * (by + 24)), BF16),
-            ((terms * wide1, 3 * (wide1 + 2 * hy)), BF16),
+            ((terms * wide1, 3 * (wide1 + 16 + 2 * tip)), BF16),
             ((terms * wide2, 3 * wy * wide2), BF16),
             ((2, terms * bz, bz), BF16),
             ((2, terms * hz, hz), BF16),
@@ -512,10 +552,11 @@
             ((2, -(-2 * (margin + 1) // 8), 8, hz), F32),
             ((2, -(-2 * (margin + 1) // 8), 8, hz), F32),
             (charges.shape, F32),
+            ((2, radius, terms, by, bz), F32),
         )
     ] + [
-        pltpu.SemaphoreType.DMA((48,)),
-        pltpu.SemaphoreType.DMA((48,)),
+        pltpu.SemaphoreType.DMA((36,)),
+        pltpu.SemaphoreType.DMA((36,)),
         pltpu.SemaphoreType.DMA((2 + len(fixed),)),
         pltpu.SemaphoreType.DMA((8,)),
     ]

time: 41.5 us -> 37.7 us (0.908)
  Pallas kernels: 41.3 us -> 37.5 us
    pallas_call x1, Pallas kernels: 39.2 us -> 35.4 us  [body(): pl.pallas_call(functools.partial(kernel, nx, ny, radius, terms), out_shap...]
where the time goes in v3:
time: 37.7 us; the launch traced here: 37.5 us
  Pallas kernels  37.5 us (99%)
    pallas_call x1, Pallas kernels, body(): pl.pallas_call(functools.partial(kernel, nx, ny, radius, terms), out_shap...  35.4 us
    pallas_call x1, Pallas kernels, body(): pl.pallas_call(functools.partial(hand_over, pieces), out_shape=jax.ShapeD...  2.09 us

profile of v3, /device:TPU:1, one launch (start us, length us, event | category | flops | bytes accessed | tf_op | source)
XLA Modules:
  0.0 37.5 jit_solution(16450563643924387112)
XLA Ops:
  0.0 35.4 %shard_map.100.source = f32[32,32,256]{2,1,0:T(8,128)} custom-call(f32[3,3,21]{2,1,0:T(4,128)} %refs_0_.1, f32[32,32,256]{2,1,0:T(8,128)} %refs_1_.1, bf16[24,64]{1,0:T(8,128)(2,1)} %constant.16.clone.refs_2_, bf16[256,128]{1,0:T(8,128)(2,1)} %constant.17.clone.refs_3_, bf16[16,48]{1,0:T(8,128)(2,1)} %constant.18.clone.refs_4_, ...), custom_call_target="tpu_custom_call" | custom-call | tf_op jit(solution)/shard_map/pallas_call | solution.py:563
  35.4 2.1 %shard_map.101 = f32[32,32,256]{2,1,0:T(8,128)} custom-call(f32[32,32,256]{2,1,0:T(8,128)} %shard_map.100.source), custom_call_target="tpu_custom_call" | custom-call | tf_op jit(solution)/shard_map/pallas_call | solution.py:574

commit v4 on v3

--- a/solution.py
+++ b/solution.py
@@ -2,7 +2,6 @@
 
 import jax
 import jax.numpy as jnp
-import numpy as np
 from jax import lax
 from jax.experimental import pallas as pl
 from jax.experimental.pallas import tpu as pltpu
@@ -11,32 +10,6 @@
 SPLINE = (0.125, 0.5, 0.75, 0.5, 0.125)
 F32, BF16 = jnp.float32, jnp.bfloat16
 MESH = pl.DeviceIdType.MESH
-
-
-def spline_at(offset):
-    return SPLINE[offset + 2] if -2 <= offset <= 2 else 0.0
-
-
-def fixed_table(rows, cols, width):
-    table = np.zeros((width, len(cols)), np.float32)
-    for a, fine in enumerate(rows):
-        for b, other in enumerate(cols):
-            if fine is not None and other is not None:
-                table[a, b] = spline_at(other - 2 * fine)
-    return table
-
-
-def lifted_table(rows, cols, width):
-    table = np.zeros((width, len(cols)), np.float32)
-    for a, fine in enumerate(rows):
-        for b, coarse in enumerate(cols):
-            if coarse is not None:
-                table[a, b] = spline_at(fine - 2 * coarse)
-    return table
-
-
-def twice(table):
-    return jnp.asarray(np.concatenate([table, table], axis=1), BF16)
 
 
 def halves(value):
@@ -69,11 +42,11 @@
 
 
 def kernel(nx, ny, radius, terms, *refs):
-    given, out, held, refs = refs[:10], refs[10], refs[11:20], refs[20:]
+    given, out, held, refs = refs[:2], refs[2], refs[3:12], refs[12:]
     taps, ry1, rz1, ry2, rz2, uy2, uz2, uy1, uz1 = held
     (fine, mid, ext, got, tips, tips_in, low1, high1, l2p, cols2, seen2, top,
            ty0, ty1, ty2, tz0, tz1, tz2, y0, s0, y1, s1, y2, s2, r1, l1w, l2y, tx, ty, md, my,
-     edge, edge_in, stage, part, send, recv, load, store) = refs
+     edge, edge_in, part, send, recv, load) = refs
     bx, by, bz = given[1].shape
     x0, x1 = radius, radius + bx
     hx, hy, hz = bx // 2, by // 2, bz // 2
@@ -102,7 +75,7 @@
 
     fetched = [
         pltpu.make_async_copy(source, target, load.at[n])
-        for n, (source, target) in enumerate(zip(given, [taps, fine.at[x0:x1, 0:by]] + list(held[1:])))
+        for n, (source, target) in enumerate(zip(given, [taps, fine.at[x0:x1, 0:by]]))
     ]
     for copy in fetched:
         copy.start()
@@ -184,6 +157,36 @@
                 total = piece if total is None else total + piece
         return total
 
+    def places(shape, axis):
+        return lax.broadcasted_iota(jnp.int32, shape, axis)
+
+    def spline_table(ref, offset, valid):
+        distance = jnp.abs(offset)
+        value = jnp.where(distance == 0, SPLINE[2], jnp.where(distance == 1, SPLINE[1], jnp.where(distance == 2, SPLINE[0], 0.0)))
+        ref[...] = jnp.where(valid, value, 0.0).astype(BF16)
+
+    def folded(index, width):
+        return jnp.where(index >= width, index - width, index)
+
+    def along_z(ref, fine_axis, n, blocks):
+        rows, cols = places(ref.shape, fine_axis), places(ref.shape, 1 - fine_axis)
+        same = (rows >= n) == (cols >= n // 2) if blocks == 2 else rows >= 0
+        offset = folded(rows, n) - 2 * folded(cols, n // 2) if blocks == 2 else rows - 2 * cols
+        offset = jnp.where(offset > n // 2, offset - n, jnp.where(offset < -(n // 2), offset + n, offset))
+        spline_table(ref, offset, same)
+
+    a, b = places(ry1.shape, 0), folded(places(ry1.shape, 1), by)
+    spline_table(ry1, b - 2 * jnp.where(a == hy + 1, -1, a), a <= hy + 1)
+    a, b = places(ry2.shape, 0), folded(places(ry2.shape, 1), ry1.shape[0])
+    spline_table(ry2, jnp.where(b == hy + 1, -1, b) - 2 * jnp.where(a == ey + 2, -1, a), (a <= ey + 2) & (b <= hy + 1))
+    a, b = places(uy2.shape, 0), folded(places(uy2.shape, 1), ry2.shape[0])
+    spline_table(uy2, a + 1 - 2 * b, (a < hy + 2) & (b < ey + 3))
+    a, b = places(uy1.shape, 0), folded(places(uy1.shape, 1), ry1.shape[0])
+    spline_table(uy1, a + 2 - 2 * b, b < hy + 2)
+    along_z(rz1, 0, bz, 1)
+    along_z(uz1, 1, bz, 1)
+    along_z(rz2, 0, hz, 2)
+    along_z(uz2, 1, hz, 1)
     for copy in fetched:
         copy.wait()
     rows1, rows2 = hx + 2, ex + 3
@@ -436,16 +439,12 @@
         my[0, j] = high
         my[1, j] = low
 
-    stored = []
-
     def finish(start, size):
         rows = span(start, size)
         high = my[0, rows].reshape(size * by, hz)
         low = my[1, rows].reshape(size * by, hz)
         total = correlate_z(s0, tz0, rows, size) + dot(high, uz1[...]) + dot(low, uz1[...])
-        stage[rows] = total.reshape(size, by, bz)
-        stored.append(pltpu.make_async_copy(stage.at[rows], out.at[rows], store.at[len(stored)]))
-        stored[-1].start()
+        out[rows] = total.reshape(size, by, bz)
 
     for copies in near:
         relay(copies)
@@ -456,8 +455,6 @@
         correlate_y(y0, fine, ty0, b - a, (b - a) // 2, halo)
         add_halo(even if n else odd, a, b)
         finish(target, b - a)
-    for copy in stored:
-        copy.wait()
     for copy in fan + rim + side + lines + sum(near, []) + far + rim2 + sum(corners, []):
         copy.wait_send()
 
@@ -465,28 +462,6 @@
 def near_steps(radius):
     first = min(radius, radius // 2 + radius // 2 % 2)
     return [(0, first), (first, radius)]
-
-
-def hand_over(pieces, source, target, held, load, store):
-    size = source.shape[0] // pieces
-    reads = [pltpu.make_async_copy(source.at[i * size : (i + 1) * size], held.at[i * size : (i + 1) * size], load.at[i]) for i in range(pieces)]
-    writes = [pltpu.make_async_copy(held.at[i * size : (i + 1) * size], target.at[i * size : (i + 1) * size], store.at[i]) for i in range(pieces)]
-    for copy in reads:
-        copy.start()
-    for before, after in zip(reads, writes):
-        before.wait()
-        after.start()
-    for copy in writes:
-        copy.wait()
-
-
-def cyclic_restrict(n):
-    rows = np.arange(n)[:, None]
-    cols = np.arange(n // 2)[None, :]
-    table = np.zeros((n, n // 2), np.float32)
-    for k in range(-2, 3):
-        table += SPLINE[k + 2] * ((2 * cols + k) % n == rows)
-    return table
 
 
 def body(charges, kernel_taps):
@@ -497,25 +472,16 @@
     bx, by, bz = charges.shape
     hx, hy, hz = bx // 2, by // 2, bz // 2
     ex, ey, ez = bx // 4, by // 4, bz // 4
-    pad = 16
     wy = min(ny, 5)
-    order1 = list(range(hy)) + [hy, -1] + [None] * 6
-    ry1 = fixed_table(order1, list(range(by)), len(order1))
-    order2 = list(range(ey)) + [ey, ey + 1, -1] + [None] * 5
-    ry2 = fixed_table(order2, order1, len(order2))
-    rz1, rz2 = cyclic_restrict(bz), cyclic_restrict(hz)
     wide1 = hy + 8
     wide2 = ey + 8
-    uy2 = lifted_table(list(range(-1, hy + 1)), list(range(-1, ey + 2)) + [None] * (wide2 - ey - 3), wide1)
-    uy1 = lifted_table(list(range(by)), list(range(-1, hy + 1)) + [None] * (wide1 - hy - 2), by)
-    fixed = [twice(ry1), jnp.asarray(rz1, BF16), twice(ry2), jnp.asarray(np.kron(np.eye(2), rz2), BF16), twice(uy2),
-             jnp.asarray(rz2.T, BF16), twice(uy1), jnp.asarray(rz1.T, BF16)]
+    tables = [(wide1, 2 * by), (bz, hz), (wide2, 2 * wide1), (2 * hz, 2 * ez), (wide1, 2 * wide2), (ez, hz), (by, 2 * wide1), (hz, bz)]
     rows1, rows2 = hx + 2, ex + 3
     half2, pairs = (rows2 + 1) // 2, (rows2 + 2 * radius + 1) // 2
     extra = radius - 8
     tip = margin - 7
     packed = bx * extra // 8 + sum(-(-(b - a) * extra // 8) for a, b in near_steps(radius) + [(0, radius)])
-    scratch = [pltpu.SMEM(kernel_taps.shape, F32)] + [pltpu.VMEM(table.shape, table.dtype) for table in fixed] + [
+    scratch = [pltpu.SMEM(kernel_taps.shape, F32)] + [pltpu.VMEM(shape, BF16) for shape in tables] + [
         pltpu.VMEM(shape, dtype)
         for shape, dtype in (
             ((bx + 2 * radius, by + 24, bz), F32),
@@ -551,38 +517,24 @@
             ((2, bx, by, hz), BF16),
             ((2, -(-2 * (margin + 1) // 8), 8, hz), F32),
             ((2, -(-2 * (margin + 1) // 8), 8, hz), F32),
-            (charges.shape, F32),
             ((2, radius, terms, by, bz), F32),
         )
     ] + [
         pltpu.SemaphoreType.DMA((36,)),
         pltpu.SemaphoreType.DMA((36,)),
-        pltpu.SemaphoreType.DMA((2 + len(fixed),)),
-        pltpu.SemaphoreType.DMA((8,)),
+        pltpu.SemaphoreType.DMA((2,)),
     ]
     result = pl.pallas_call(
         functools.partial(kernel, nx, ny, radius, terms),
         out_shape=jax.ShapeDtypeStruct(charges.shape, F32),
-        in_specs=[pl.BlockSpec(memory_space=pltpu.HBM)] * (2 + len(fixed)),
-        out_specs=pl.BlockSpec(memory_space=pltpu.HBM),
+        in_specs=[pl.BlockSpec(memory_space=pltpu.HBM)] * 2,
+        out_specs=pl.BlockSpec(memory_space=pltpu.VMEM),
         scratch_shapes=scratch,
         compiler_params=pltpu.CompilerParams(
-            collective_id=0, has_side_effects=True, vmem_limit_bytes=60 * 2**20
+            collective_id=0, has_side_effects=True, vmem_limit_bytes=211 * 2**18
         ),
-    )(kernel_taps, charges, *fixed)
-    pieces = 8
-    return pl.pallas_call(
-        functools.partial(hand_over, pieces),
-        out_shape=jax.ShapeDtypeStruct(charges.shape, F32),
-        in_specs=[pl.BlockSpec(memory_space=pltpu.HBM)],
-        out_specs=pl.BlockSpec(memory_space=pltpu.HBM),
-        scratch_shapes=[
-            pltpu.VMEM(charges.shape, F32),
-            pltpu.SemaphoreType.DMA((pieces,)),
-            pltpu.SemaphoreType.DMA((pieces,)),
-        ],
-        compiler_params=pltpu.CompilerParams(vmem_limit_bytes=60 * 2**20),
-    )(result)
+    )(kernel_taps, charges)
+    return result
 
 
 def solution(mesh):

time: 37.7 us -> 36.4 us (0.966)
  Pallas kernels: 37.5 us -> 34.6 us
  local copies, waits for them, and re-layouts: 0 us -> 1.66 us
    pallas_call x1 -> x0, Pallas kernels: 2.09 us -> none  [body(): pl.pallas_call(functools.partial(hand_over, pieces), out_shape=jax.ShapeD...]
    unnamed x0 -> x3, local copies, waits for them, and re-layouts: none -> 1.66 us
    pallas_call x1, Pallas kernels: 35.4 us -> 34.6 us  [body(): pl.pallas_call(functools.partial(kernel, nx, ny, radius, terms), out_shap...]
where the time goes in v4:
time: 36.4 us; the launch traced here: 36.3 us
  Pallas kernels  34.6 us (95%)
  local copies, waits for them, and re-layouts  1.66 us (5%)
    pallas_call x1, Pallas kernels, body(): pl.pallas_call(functools.partial(kernel, nx, ny, radius, terms), out_shap...  34.6 us
    unnamed x3, local copies, waits for them, and re-layouts  1.66 us

profile of v4, /device:TPU:1, one launch (start us, length us, event | category | flops | bytes accessed | tf_op | source)
XLA Modules:
  0.0 36.3 jit_solution(7377689624993644029)
XLA Ops:
  0.0 0.0 copy-start
  0.0 0.7 %copy-done = f32[3,3,21]{2,1,0:T(4,128)S(1)} copy-done((f32[3,3,21]{2,1,0:T(4,128)S(1)}, f32[3,3,21]{2,1,0:T(4,128)}, u32[]{:S(2)}) %copy-start) | copy-done | bytes 780
  0.7 34.6 %shard_map.28 = f32[32,32,256]{2,1,0:T(8,128)S(1)} custom-call(f32[3,3,21]{2,1,0:T(4,128)S(1)} %copy-done, f32[32,32,256]{2,1,0:T(8,128)} %refs_1_.1), custom_call_target="tpu_custom_call" | custom-call | tf_op jit(solution)/shard_map/pallas_call | solution.py:527
  35.3 1.0 %copy.4 = f32[32,32,256]{2,1,0:T(8,128)} copy(f32[32,32,256]{2,1,0:T(8,128)S(1)} %shard_map.28) | data formatting | bytes 2097152
Async XLA Ops:
  0.0 0.7 %copy-start = (f32[3,3,21]{2,1,0:T(4,128)S(1)}, f32[3,3,21]{2,1,0:T(4,128)}, u32[]{:S(2)}) copy-start(f32[3,3,21]{2,1,0:T(4,128)} %refs_0_.1) | copy-start | bytes 2272

commit v5 on v4

--- a/solution.py
+++ b/solution.py
@@ -333,7 +333,10 @@
             tips[d, g, r : r + tip - 1] = mid[i, a:b]
             tips[d, g, r + tip - 1 : r + tip] = mid[i, hy + d : hy + d + 1]
     rim2 += both([remote(tips.at[d], tips_in.at[d], 0, dy) for d, dy in ((0, 1), (1, -1))])
-    far = both([remote(fine.at[span(pick(x0, x1 - radius), radius), 0:by], fine.at[span(pick(x1, 0), radius), 0:by], odd - even, 0)])
+    far = [
+        both([remote(fine.at[span(pick(x0 + a, x1 - b), b - a), 0:by], fine.at[span(pick(x1 + a, x0 - b), b - a), 0:by], odd - even, 0)])
+        for a, b in steps
+    ]
 
     def correlate_z(ref, table, rows, count):
         size = count * ref.shape[2]
@@ -397,17 +400,17 @@
             remote(ext.at[1, groups], got.at[1, groups], 0, -1),
         ])
 
-    parts = [(0, radius, pick(0, x1), pick(0, bx - radius))] + [
-        (a, b, pick(x1 + a, x0 - b), pick(bx - radius + a, radius - b)) for a, b in steps
+    parts = [(a, b, pick(x0 - b, x1 + a), pick(radius - b, bx - radius + a), odd) for a, b in steps] + [
+        (a, b, pick(x1 + a, x0 - b), pick(bx - radius + a, radius - b), even) for a, b in steps
     ]
     groups = [g1]
-    for a, b, _, _ in parts:
+    for a, b, _, _, _ in parts:
         groups.append(groups[-1] + -(-(b - a) // per))
     corners = []
 
     def relay(copies):
         n = len(corners)
-        a, b, halo, _ = parts[n]
+        a, b, halo, _, _ = parts[n]
         arrive(copies)
         corners.append(pack(halo, b - a, groups[n]))
 
@@ -425,14 +428,17 @@
     lifted = dot(high, uz2[...]) + dot(low, uz2[...])
 
     md[...] = lifted.reshape(md.shape)
+    relay(far[0])
     arrive(rim2)
     for i in range(mid.shape[0]):
         g, r = i // tip_per, tip * (i % tip_per)
         for d in range(2):
             mid[i, wide1 + 16 + tip * d : wide1 + 16 + tip * (d + 1)] = tips_in[d, g, r : r + tip]
     correlate_y(y1, mid, ty1, hx + 2 * margin, (hx + 2 * margin) // 2)
-    correlate_x(s1, y1, 1, hx + 2, 0, 1)
-    relay(far)
+    early = (hx + 2) // 2
+    correlate_x(s1, y1, 1, early, 0, 1)
+    relay(far[1])
+    correlate_x(s1, y1, 1, hx + 2 - early, 0, 1, early)
     md[...] += correlate_z(s1, tz1, slice(0, hx + 2), hx + 2).reshape(md.shape)
     for j in range(bx):
         high, low = halves(dot(uy1[...], stacked2(prolong_x(md, j, -1))))
@@ -446,16 +452,17 @@
         total = correlate_z(s0, tz0, rows, size) + dot(high, uz1[...]) + dot(low, uz1[...])
         out[rows] = total.reshape(size, by, bz)
 
-    for copies in near:
-        relay(copies)
+    relay(near[0])
     finish(radius, bx - 2 * radius)
-    for n, (a, b, halo, target) in enumerate(parts):
+    for n, (a, b, halo, target, edge_of) in enumerate(parts):
         arrive(corners[n])
         unpack([halo + k for k in range(b - a)], groups[n])
         correlate_y(y0, fine, ty0, b - a, (b - a) // 2, halo)
-        add_halo(even if n else odd, a, b)
+        add_halo(edge_of, a, b)
+        if n == 0:
+            relay(near[1])
         finish(target, b - a)
-    for copy in fan + rim + side + lines + sum(near, []) + far + rim2 + sum(corners, []):
+    for copy in fan + rim + side + lines + sum(near + far, []) + rim2 + sum(corners, []):
         copy.wait_send()
 
 
@@ -480,7 +487,7 @@
     half2, pairs = (rows2 + 1) // 2, (rows2 + 2 * radius + 1) // 2
     extra = radius - 8
     tip = margin - 7
-    packed = bx * extra // 8 + sum(-(-(b - a) * extra // 8) for a, b in near_steps(radius) + [(0, radius)])
+    packed = bx * extra // 8 + sum(-(-(b - a) * extra // 8) for a, b in 2 * near_steps(radius))
     scratch = [pltpu.SMEM(kernel_taps.shape, F32)] + [pltpu.VMEM(shape, BF16) for shape in tables] + [
         pltpu.VMEM(shape, dtype)
         for shape, dtype in (
@@ -520,8 +527,8 @@
             ((2, radius, terms, by, bz), F32),
         )
     ] + [
-        pltpu.SemaphoreType.DMA((36,)),
-        pltpu.SemaphoreType.DMA((36,)),
+        pltpu.SemaphoreType.DMA((40,)),
+        pltpu.SemaphoreType.DMA((40,)),
         pltpu.SemaphoreType.DMA((2,)),
     ]
     result = pl.pallas_call(

time: 36.4 us -> 34.9 us (0.959)
  Pallas kernels: 34.6 us -> 33.1 us
    pallas_call x1, Pallas kernels: 34.6 us -> 33.1 us  [body(): pl.pallas_call(functools.partial(kernel, nx, ny, radius, terms), out_shap...]
where the time goes in v5:
time: 34.9 us; the launch traced here: 34.7 us
  Pallas kernels  33.1 us (95%)
  local copies, waits for them, and re-layouts  1.66 us (5%)
    pallas_call x1, Pallas kernels, body(): pl.pallas_call(functools.partial(kernel, nx, ny, radius, terms), out_shap...  33.1 us
    unnamed x3, local copies, waits for them, and re-layouts  1.66 us

profile of v5, /device:TPU:1, one launch (start us, length us, event | category | flops | bytes accessed | tf_op | source)
XLA Modules:
  0.0 34.7 jit_solution(2265735170461428865)
XLA Ops:
  0.0 0.0 copy-start
  0.0 0.7 %copy-done = f32[3,3,21]{2,1,0:T(4,128)S(1)} copy-done((f32[3,3,21]{2,1,0:T(4,128)S(1)}, f32[3,3,21]{2,1,0:T(4,128)}, u32[]{:S(2)}) %copy-start) | copy-done | bytes 780
  0.7 33.1 %shard_map.28 = f32[32,32,256]{2,1,0:T(8,128)S(1)} custom-call(f32[3,3,21]{2,1,0:T(4,128)S(1)} %copy-done, f32[32,32,256]{2,1,0:T(8,128)} %refs_1_.1), custom_call_target="tpu_custom_call" | custom-call | tf_op jit(solution)/shard_map/pallas_call | solution.py:534
  33.8 1.0 %copy.4 = f32[32,32,256]{2,1,0:T(8,128)} copy(f32[32,32,256]{2,1,0:T(8,128)S(1)} %shard_map.28) | data formatting | bytes 2097152
Async XLA Ops:
  0.0 0.7 %copy-start = (f32[3,3,21]{2,1,0:T(4,128)S(1)}, f32[3,3,21]{2,1,0:T(4,128)}, u32[]{:S(2)}) copy-start(f32[3,3,21]{2,1,0:T(4,128)} %refs_0_.1) | copy-start | bytes 2272

commit v6 on v5

--- a/solution.py
+++ b/solution.py
@@ -420,7 +420,7 @@
         for member in range(terms):
             y2[member, j] = value[member * wide2 : (member + 1) * wide2, 0:ez]
             y2[member, j + pairs] = value[member * wide2 : (member + 1) * wide2, ez : 2 * ez]
-    correlate_x(s2, y2, 2, rows2, 0, 1)
+    correlate_x(s2, y2, 2, rows2, 0, rows2)
     tx[...] = correlate_z(s2, tz2, slice(0, rows2), rows2).reshape(tx.shape)
     for j in range(hx + 2):
         ty[j] = dot(uy2[...], stacked2(prolong_x(tx, j - 1, -1)))
@@ -440,10 +440,12 @@
     relay(far[1])
     correlate_x(s1, y1, 1, hx + 2 - early, 0, 1, early)
     md[...] += correlate_z(s1, tz1, slice(0, hx + 2), hx + 2).reshape(md.shape)
-    for j in range(bx):
-        high, low = halves(dot(uy1[...], stacked2(prolong_x(md, j, -1))))
-        my[0, j] = high
-        my[1, j] = low
+    for j in range(0, bx, 2):
+        pair = jnp.concatenate([prolong_x(md, j, -1), prolong_x(md, j + 1, -1)], axis=1)
+        high, low = halves(dot(uy1[...], stacked2(pair)))
+        for k in range(2):
+            my[0, j + k] = high[:, k * hz : (k + 1) * hz]
+            my[1, j + k] = low[:, k * hz : (k + 1) * hz]
 
     def finish(start, size):
         rows = span(start, size)

time: 34.9 us -> 34.4 us (0.986)
  Pallas kernels: 33.1 us -> 32.6 us
    pallas_call x1, Pallas kernels: 33.1 us -> 32.6 us  [body(): pl.pallas_call(functools.partial(kernel, nx, ny, radius, terms), out_shap...]
where the time goes in v6:
time: 34.4 us; the launch traced here: 34.3 us
  Pallas kernels  32.6 us (95%)
  local copies, waits for them, and re-layouts  1.66 us (5%)
    pallas_call x1, Pallas kernels, body(): pl.pallas_call(functools.partial(kernel, nx, ny, radius, terms), out_shap...  32.6 us
    unnamed x3, local copies, waits for them, and re-layouts  1.66 us

profile of v6, /device:TPU:1, one launch (start us, length us, event | category | flops | bytes accessed | tf_op | source)
XLA Modules:
  0.0 34.3 jit_solution(5486389313868397690)
XLA Ops:
  0.0 0.0 copy-start
  0.0 0.7 %copy-done = f32[3,3,21]{2,1,0:T(4,128)S(1)} copy-done((f32[3,3,21]{2,1,0:T(4,128)S(1)}, f32[3,3,21]{2,1,0:T(4,128)}, u32[]{:S(2)}) %copy-start) | copy-done | bytes 780
  0.7 32.6 %shard_map.28 = f32[32,32,256]{2,1,0:T(8,128)S(1)} custom-call(f32[3,3,21]{2,1,0:T(4,128)S(1)} %copy-done, f32[32,32,256]{2,1,0:T(8,128)} %refs_1_.1), custom_call_target="tpu_custom_call" | custom-call | tf_op jit(solution)/shard_map/pallas_call | solution.py:536
  33.3 1.0 %copy.4 = f32[32,32,256]{2,1,0:T(8,128)} copy(f32[32,32,256]{2,1,0:T(8,128)S(1)} %shard_map.28) | data formatting | bytes 2097152
Async XLA Ops:
  0.0 0.7 %copy-start = (f32[3,3,21]{2,1,0:T(4,128)S(1)}, f32[3,3,21]{2,1,0:T(4,128)}, u32[]{:S(2)}) copy-start(f32[3,3,21]{2,1,0:T(4,128)} %refs_0_.1) | copy-start | bytes 2272

commit v7 on v6

--- a/solution.py
+++ b/solution.py
@@ -436,9 +436,9 @@
             mid[i, wide1 + 16 + tip * d : wide1 + 16 + tip * (d + 1)] = tips_in[d, g, r : r + tip]
     correlate_y(y1, mid, ty1, hx + 2 * margin, (hx + 2 * margin) // 2)
     early = (hx + 2) // 2
-    correlate_x(s1, y1, 1, early, 0, 1)
+    correlate_x(s1, y1, 1, early, 0, early)
     relay(far[1])
-    correlate_x(s1, y1, 1, hx + 2 - early, 0, 1, early)
+    correlate_x(s1, y1, 1, hx + 2 - early, 0, hx + 2 - early, early)
     md[...] += correlate_z(s1, tz1, slice(0, hx + 2), hx + 2).reshape(md.shape)
     for j in range(0, bx, 2):
         pair = jnp.concatenate([prolong_x(md, j, -1), prolong_x(md, j + 1, -1)], axis=1)

time: 34.4 us -> 34.6 us (level)
  no operation moved by 1% of the time
where the time goes in v7:
time: 34.6 us; the launch traced here: 34.5 us
  Pallas kernels  32.8 us (95%)
  local copies, waits for them, and re-layouts  1.66 us (5%)
    pallas_call x1, Pallas kernels, body(): pl.pallas_call(functools.partial(kernel, nx, ny, radius, terms), out_shap...  32.8 us
    unnamed x3, local copies, waits for them, and re-layouts  1.66 us

profile of v7, /device:TPU:1, one launch (start us, length us, event | category | flops | bytes accessed | tf_op | source)
XLA Modules:
  0.0 34.5 jit_solution(6009264933502753645)
XLA Ops:
  0.0 0.0 copy-start
  0.0 0.7 %copy-done = f32[3,3,21]{2,1,0:T(4,128)S(1)} copy-done((f32[3,3,21]{2,1,0:T(4,128)S(1)}, f32[3,3,21]{2,1,0:T(4,128)}, u32[]{:S(2)}) %copy-start) | copy-done | bytes 780
  0.7 32.8 %shard_map.28 = f32[32,32,256]{2,1,0:T(8,128)S(1)} custom-call(f32[3,3,21]{2,1,0:T(4,128)S(1)} %copy-done, f32[32,32,256]{2,1,0:T(8,128)} %refs_1_.1), custom_call_target="tpu_custom_call" | custom-call | tf_op jit(solution)/shard_map/pallas_call | solution.py:536
  33.5 1.0 %copy.4 = f32[32,32,256]{2,1,0:T(8,128)} copy(f32[32,32,256]{2,1,0:T(8,128)S(1)} %shard_map.28) | data formatting | bytes 2097152
Async XLA Ops:
  0.0 0.7 %copy-start = (f32[3,3,21]{2,1,0:T(4,128)S(1)}, f32[3,3,21]{2,1,0:T(4,128)}, u32[]{:S(2)}) copy-start(f32[3,3,21]{2,1,0:T(4,128)} %refs_0_.1) | copy-start | bytes 2272
